TPU v7x, 1024 devices: a whole 4x8x16 slice. The times are simulated.
1024 devices in a mesh: group: 4 (over z_lo), seq: 32 (over z_hi, y), shard: 8 (over x, core).
Axes of the slice: x: 4, y: 8, z: 16 (z_hi: 4, z_lo: 4; z = z_hi * 4 + z_lo), core: 2. Of those that a mesh axis runs over, the one named last changes fastest.
Arguments:
- text_rows: bfloat16 [32768, 8, 1280], P(('group', 'seq'), 'shard'), may hold values from -64 to 64
- vis_rows: bfloat16 [8192, 8, 1280], P(('group', 'seq', 'shard')), may hold values from -6 to 6
- vis_dest: int32 [8192, 1], P(('group', 'seq', 'shard')), may hold values from 0 to 31; in each aligned block of 64 rows (0 to 63, 64 to 127, ...) at most 4 rows name the same one
- segments: int32 [49152], P(('group', 'seq')), may hold values from 0 to 63, never falling along the last dimension, each value on 1 to 1536 neighbouring positions
Outputs:
- attended: bfloat16 [49152, 8, 1024], P(('group', 'seq'), 'shard')
Inputs may be any that keep to these rules, and one draw needn't show every extreme that they name: `vis_dest`: in each aligned block of 64 rows (the visual rows listed by one index of group and seq, in device order), no value is named by more than 4 rows, and this bound is reached. `segments`: ids never fall along the sequence; each document covers 1 to 1536 positions, and one covers exactly 1536.
All inputs are finite; a program needn't handle non-finite values.
Results may differ from a plain program's by a relative error of at most 0.0028.
Values may be sent and summed in bfloat16 or wider, within the bound.
No kernel may reach another device: no remote copies, remote signals or barrier semaphores. Data moves between devices by JAX's collectives and lax.ppermute only.
A program may use at most 32 MiB of HBM per device.

v0:
```python
import functools

import jax
import jax.numpy as jnp
from jax import lax
from jax.experimental import pallas as pl
from jax.experimental.pallas import tpu as pltpu
from jax.sharding import PartitionSpec as P


GQ = 8
DH = 128
CAP = 4
REACH = 4
RING = 8
LANES = 128
DEAD = 64.0
BIG = 1e30
SCALE = DH ** (-0.5) * 1.4426950408889634
F32 = jnp.float32
BF16 = jnp.bfloat16

VARIANTS = (1, 3, 5)


def iota(shape, dim):
    return lax.broadcasted_iota(jnp.int32, shape, dim)


def dot(a, b):
    return jnp.dot(a, b, preferred_element_type=F32)


def dot_nt(a, b):
    return lax.dot_general(a, b, (((1,), (1,)), ((), ())), preferred_element_type=F32)


def ones_where(cond):
    return jnp.where(cond, 1.0, 0.0)


def halo_kernel(text_ref, vis_ref, dest_ref, seg_ref, mine_ref, step_ref):
    text = text_ref.shape[0]
    block = vis_ref.shape[0]
    wide = text_ref.shape[1]
    rows = seg_ref.shape[1]
    per_dev = dest_ref.shape[1]
    mine_ref[:text] = text_ref[...]
    tags = seg_ref[...].astype(F32) + 1.0
    pad = jnp.zeros((1, 2 * wide - rows), F32)
    tags = jnp.concatenate([tags, pad], axis=1)
    tags = jnp.concatenate([tags[:, :wide], tags[:, wide:], jnp.zeros((6, wide), F32)], axis=0)
    mine_ref[text:] = tags.astype(BF16)
    step_ref[:block] = vis_ref[...]
    dest = jnp.concatenate([dest_ref[...].astype(F32), jnp.zeros((1, wide - per_dev), F32)], axis=1)
    step_ref[block:] = jnp.broadcast_to(dest, (8, wide)).astype(BF16)


def list_kernel(per_dev, heads, rows_ref, dest_ref, step_ref, out_ref):
    count = per_dev * heads
    wide = rows_ref.shape[1]
    a, b = iota((count, count), 0), iota((count, count), 1)
    move = ones_where(b == (a % per_dev) * heads + a // per_dev).astype(BF16)
    pick = iota((count, per_dev), 1) == iota((count, per_dev), 0) % per_dev
    dest = jnp.sum(jnp.where(pick, dest_ref[...].astype(F32), 0.0), axis=1, keepdims=True)
    old = jnp.sum(jnp.where(pick, step_ref[count : count + 1, :per_dev].astype(F32), 0.0), axis=1, keepdims=True)
    out_ref[:, :wide] = dot(move, rows_ref[...]).astype(BF16)
    out_ref[:, wide : wide + LANES] = jnp.broadcast_to(dest, (count, LANES)).astype(BF16)
    out_ref[:, wide + LANES : wide + LANES + 2 * DH] = dot(move, step_ref[:count]).astype(BF16)
    out_ref[:, wide + LANES + 2 * DH :] = jnp.broadcast_to(old, (count, LANES)).astype(BF16)


def slot_row(named):
    count = named.shape[0]
    onehot = ones_where(named.astype(F32).astype(jnp.int32) == iota((count, LANES), 1)).astype(BF16)
    same = dot_nt(onehot, onehot)
    a, b = iota((count, count), 0), iota((count, count), 1)
    rank = jnp.sum(jnp.where(a < b, same, 0.0), axis=0, keepdims=True)
    dest = dot_nt(iota((8, LANES), 1).astype(F32).astype(BF16), onehot)[0:1]
    return dest * CAP + rank


def pack_kernel(own_ref, out_ref):
    count = own_ref.shape[0]
    rows = out_ref.shape[0]
    slot_count = rows // 2
    q = GQ * DH
    wide = q + 2 * DH
    slots = slot_row(own_ref[:, wide : wide + LANES])
    before = slot_row(own_ref[:, wide + LANES + 2 * DH :]) - slot_count
    both = jnp.concatenate([slots, before], axis=1)
    kv = jnp.concatenate([own_ref[:, q:wide], own_ref[:, wide + LANES : wide + LANES + 2 * DH]], axis=0)
    r = iota((rows, count), 0)
    sid = ((r // 8) * CAP + r % CAP).astype(F32)
    low = (r % 8) < CAP
    put0 = ones_where(low & (sid == slots))
    put1 = ones_where((~low) & (sid == slots))
    base = dot(put0.astype(BF16), own_ref[:, : q + DH])
    fill0 = jnp.sum(put0, axis=1, keepdims=True)
    first = base[:, :DH] + dot(put1.astype(BF16), own_ref[:, q + DH : wide])
    fill = fill0 + jnp.sum(put1, axis=1, keepdims=True)
    out_ref[:, :DH] = jnp.where(fill > 0, first, DEAD).astype(BF16)
    r = iota((rows, 2 * count), 0)
    sid = ((r // 8) * CAP + r % CAP).astype(F32)
    low = (r % 8) < CAP
    for k in range(1, REACH + 1):
        put = ones_where((~low) & (sid - CAP * k == both))
        lo = DH + 2 * DH * (k - 1)
        val = base[:, lo : lo + 2 * DH] + dot(put.astype(BF16), kv)
        fill = fill0 + jnp.sum(put, axis=1, keepdims=True)
        out_ref[:, lo : lo + 2 * DH] = jnp.where(fill > 0, val, DEAD).astype(BF16)


def attend_kernel(text_ref, seg_ref, came_ref, b1, b2, b3, far, c1, c2, c3, out_ref, qv, kk, vv, qx, own_bias, sa, sb):
    text = text_ref.shape[0]
    vis = came_ref.shape[0] // 2
    rows = text + vis
    q = GQ * DH
    a, b = iota((vis, 2 * vis), 0), iota((vis, 2 * vis), 1)
    src = (a // CAP) * 8 + a % CAP
    low = dot(ones_where(b == src).astype(BF16), came_ref[...])
    high = dot(ones_where(b == src + CAP).astype(BF16), came_ref[...])
    qv[...] = low[:, :q].astype(BF16)
    own_k = low[:, q:].astype(BF16)
    kk[:text, :DH] = text_ref[:, q : q + DH]
    kk[text:rows, :DH] = own_k
    kk[:rows, DH:] = jnp.zeros((rows, LANES), BF16)
    vv[:text, :DH] = text_ref[:, q + DH :]
    vv[text:rows, :DH] = high[:, :DH].astype(BF16)
    vv[:, DH:] = jnp.ones((vv.shape[0], DH), BF16)
    tags = jnp.broadcast_to(seg_ref[0:1].astype(F32) + 1.0, (8, rows))
    first_tag = tags[0:1, 0:1]
    diag = ones_where(iota((rows, rows), 0) == iota((rows, rows), 1)) * tags[0:1]
    tag_col = dot(diag.astype(BF16), jnp.ones((rows, LANES), BF16))
    pick0 = ones_where(iota((8, DH), 1) == 0).astype(BF16)
    vis_live = ones_where(dot_nt(pick0, own_k)[0:1] < DEAD / 2)
    live_lane = jnp.concatenate([jnp.ones((1, text), F32), vis_live], axis=1)
    a, b = iota((rows, rows), 0), iota((rows, rows), 1)
    tag_wide = jnp.concatenate([tag_col] * (rows // LANES), axis=1)
    seen = (b <= a) & (tag_wide == tags[0:1]) & (live_lane > 0.5)
    own_bias[...] = jnp.where(seen, 0.0, -BIG)
    lane = iota((rows, LANES), 1)
    row_bias = jnp.where(tag_col == first_tag, 0.0, -BIG)
    qx[...] = jnp.where(lane == 0, 1.0, jnp.where(lane == 1, row_bias, 0.0)).astype(BF16)
    live_q = jnp.concatenate(
        [jnp.ones((text, LANES), F32), jnp.broadcast_to(ones_where(low[:, q : q + 1] < DEAD / 2), (vis, LANES))], axis=0
    )
    used = jnp.int32(0)
    place_r = iota((rows, LANES), 0)
    for k in range(1, REACH + 1):
        ref = far[...] if k == REACH else (b1, b2, b3)[k - 1][...] + (c1, c2, c3)[k - 1][...]
        got = ref[text : text + 8, :].astype(F32)
        same = ones_where(got == first_tag)
        count = jnp.sum(same[0:1] + same[1:2])
        at = k * rows
        lo = DH + 2 * DH * (k - 1)
        pk = high[:, lo : lo + DH]
        kk[at : at + text, :DH] = ref[:text, :DH]
        kk[at + text : at + rows, :DH] = pk.astype(BF16)
        vv[at : at + text, :DH] = ref[:text, DH:]
        vv[at + text : at + rows, :DH] = high[:, lo + DH : lo + 2 * DH].astype(BF16)
        live = jnp.concatenate(
            [jnp.ones((text, LANES), F32), jnp.broadcast_to(ones_where(pk[:, 0:1] < DEAD / 2), (vis, LANES))], axis=0
        )
        ok = (place_r >= rows - count.astype(jnp.int32)) & (live > 0.5)
        kk[at : at + rows, DH:] = jnp.where(lane == 0, jnp.where(ok, 0.0, -BIG), ones_where(lane == 1)).astype(BF16)
        used = used + jnp.where(count > 0.5, 1, 0)

    def score(h, blocks, ss):
        at = pl.multiple_of(h * DH, DH)
        qs = jnp.concatenate([text_ref[:, pl.ds(at, DH)], qv[:, pl.ds(at, DH)]], axis=0)
        qe = jnp.concatenate([qs, qx[...]], axis=1)
        top = None
        for k in range(blocks):
            s = dot_nt(qe, kk[k * rows : (k + 1) * rows])
            if k == 0:
                s = s + own_bias[...]
            ss[:, k * rows : (k + 1) * rows] = s
            for i in range(rows // LANES):
                part = s[:, i * LANES : (i + 1) * LANES]
                top = part if top is None else jnp.maximum(top, part)
        return jnp.max(top, axis=1, keepdims=True)

    def weigh(h, blocks, ss, top):
        at = pl.multiple_of(h * DH, DH)
        p = jnp.exp2((ss[:, : blocks * rows] - top) * SCALE).astype(BF16)
        acc = dot(p, vv[: blocks * rows])
        out = acc[:, :DH] / acc[:, DH:]
        out_ref[:, pl.ds(at, DH)] = jnp.where(live_q > 0.5, out, 0.0).astype(BF16)

    def run(blocks):
        def two(i, top):
            h = 2 * i
            after = score(h + 1, blocks, sb)
            weigh(h, blocks, sa, top)
            top = score(jnp.minimum(h + 2, GQ - 1), blocks, sa)
            weigh(h + 1, blocks, sb, after)
            return top

        lax.fori_loop(0, GQ // 2, two, score(0, blocks, sa))

    for blocks in VARIANTS:
        lower = max([b for b in VARIANTS if b < blocks], default=0)

        @pl.when((used + 1 > lower) & (used + 1 <= blocks))
        def _(blocks=blocks):
            run(blocks)


def cost(flops, nbytes):
    return pl.CostEstimate(flops=flops, bytes_accessed=nbytes, transcendentals=0)


def vmem(mib):
    return pltpu.CompilerParams(vmem_limit_bytes=mib << 20)


def layer(text_rows, vis_rows, vis_dest, segments):
    seq_count = lax.axis_size("seq")
    groups = lax.axis_size("group")
    text, _, wide = text_rows.shape
    per_dev, heads, _ = vis_rows.shape
    block = per_dev * heads
    vis = seq_count * CAP
    rows = text + vis
    q = GQ * DH
    total = groups * seq_count

    text2 = text_rows.reshape(text, wide)
    vis2 = vis_rows.reshape(block, wide)
    dest = vis_dest.reshape(1, per_dev)
    tail_block = q // (2 * DH)
    mine, step = pl.pallas_call(
        halo_kernel,
        grid=(1,),
        in_specs=[
            pl.BlockSpec((text, 2 * DH), lambda i: (0, tail_block)),
            pl.BlockSpec((block, 2 * DH), lambda i: (0, tail_block)),
            pl.BlockSpec((1, per_dev), lambda i: (0, 0)),
            pl.BlockSpec((1, rows), lambda i: (0, 0)),
        ],
        out_specs=[
            pl.BlockSpec((text + 8, 2 * DH), lambda i: (0, 0)),
            pl.BlockSpec((block + 8, 2 * DH), lambda i: (0, 0)),
        ],
        out_shape=[
            jax.ShapeDtypeStruct((text + 8, 2 * DH), BF16),
            jax.ShapeDtypeStruct((block + 8, 2 * DH), BF16),
        ],
        cost_estimate=cost(1000, 300_000),
        compiler_params=vmem(8),
        name="halo_rows",
    )(text2, vis2, dest, segments.reshape(1, rows))
    step = lax.ppermute(step, "group", [(i, i + 1) for i in range(groups - 1)])

    far = lax.ppermute(mine, ("group", "seq"), [(o, o + REACH) for o in range(total - REACH)])
    near, seam = [], []
    for k in range(1, REACH):
        pairs = [(s, s + k) for s in range(seq_count) if s % RING + k < RING]
        near.append(lax.ppermute(mine, "seq", pairs))
    for k in range(1, REACH):
        pairs = [(s + REACH - k, s) for s in range(seq_count) if s % RING < k]
        seam.append(lax.ppermute(far, "seq", pairs))

    listed = pl.pallas_call(
        functools.partial(list_kernel, per_dev, heads),
        out_shape=jax.ShapeDtypeStruct((block, wide + 2 * DH + 2 * LANES), BF16),
        cost_estimate=cost(15_000_000, 400_000),
        compiler_params=vmem(8),
        name="list_rows",
    )(vis2, dest, step)
    own = lax.all_to_all(listed, "shard", split_axis=0, concat_axis=0, tiled=True)

    packed = pl.pallas_call(
        pack_kernel,
        out_shape=jax.ShapeDtypeStruct((seq_count * 8, DH + 2 * DH * REACH), BF16),
        cost_estimate=cost(200_000_000, 800_000),
        compiler_params=vmem(12),
        name="pack_rows",
    )(own)
    came = lax.all_to_all(packed, "seq", split_axis=0, concat_axis=0, tiled=True)

    out = pl.pallas_call(
        attend_kernel,
        out_shape=jax.ShapeDtypeStruct((rows, q), BF16),
        scratch_shapes=[
            pltpu.VMEM((vis, q), BF16),
            pltpu.VMEM(((REACH + 1) * rows, DH + LANES), BF16),
            pltpu.VMEM(((REACH + 1) * rows, 2 * DH), BF16),
            pltpu.VMEM((rows, LANES), BF16),
            pltpu.VMEM((rows, rows), F32),
            pltpu.VMEM((rows, (REACH + 1) * rows), F32),
            pltpu.VMEM((rows, (REACH + 1) * rows), F32),
        ],
        cost_estimate=cost(6_000_000_000, 4_000_000),
        compiler_params=vmem(32),
        name="attend",
    )(text2, segments.reshape(1, rows), came, *near, far, *seam)
    return out.reshape(rows, 1, q)


def solution(mesh):
    placed = (
        P(("group", "seq"), "shard", None),
        P(("group", "seq", "shard"), None, None),
        P(("group", "seq", "shard"), None),
        P(("group", "seq")),
    )
    return jax.shard_map(
        layer,
        mesh=mesh,
        in_specs=placed,
        out_specs=P(("group", "seq"), "shard", None),
        check_vma=False,
    )
```

profile of v0, /device:TPU:448, one launch (start us, length us, event | category | flops | bytes accessed | tf_op | source)
XLA Modules:
  0.0 113.5 jit_solution(4523139695726053928)
XLA Ops:
  0.0 0.7 reshape.21.seg_ref
  0.7 0.0 copy-start.3
  0.7 0.7 copy-done.3
  1.3 0.0 copy-start
  1.3 1.1 copy-done
  2.4 0.0 copy-start.2
  2.4 0.9 copy-done.2
  3.4 1.3 %collective-permute-start = (bf16[72,256]{1,0:T(8,128)(2,1)S(1)}, bf16[72,256]{1,0:T(8,128)(2,1)S(1)}, u32[]{:S(2)}, u32[]{:S(2)}) collective-permute-start(bf16[72,256]{1,0:T(8,128)(2,1)S(1)} %get-tuple-element.7), channel_id=1, source_target_pairs={{0,256},{256,512},{512,768},{1,257},{257,513},{513,769},{2,258},{2... | collective-permute-start | bytes 110600 | tf_op jit(solution)/shard_map/ppermute | solution.py:254
  4.7 4.6 %collective-permute-done.step_ref = bf16[72,256]{1,0:T(8,128)(2,1)S(1)} collective-permute-done((bf16[72,256]{1,0:T(8,128)(2,1)S(1)}, bf16[72,256]{1,0:T(8,128)(2,1)S(1)}, u32[]{:S(2)}, u32[]{:S(2)}) %collective-permute-start) | collective-permute-done | bytes 36896 | tf_op jit(solution)/shard_map/ppermute | solution.py:254
  9.2 0.2 list_rows.1
  9.4 11.3 %all_to_all.22 = bf16[8,8,1792]{2,1,0:T(8,128)(2,1)S(1)} all-to-all(bf16[8,8,1792]{2,1,0:T(8,128)(2,1)S(1)} %bitcast.8), channel_id=1, replica_groups=mesh['group'=4,'seq'=32,'shard'=8] {'shard'}, dimensions={0} | all-to-all | bytes 458752 | tf_op jit(solution)/shard_map/all_to_all | solution.py:272
  20.7 1.4 %pack_rows.1 = bf16[256,1152]{1,0:T(8,128)(2,1)} custom-call(bf16[64,1792]{1,0:T(8,128)(2,1)S(1)} %bitcast.9), custom_call_target="tpu_custom_call" | custom-call | flops 200000000 | bytes 800000 | tf_op jit(solution)/shard_map/pack_rows/pallas_call | solution.py:274
  22.1 0.0 copy-start.1
  22.1 18.5 %all-to-all-start.1 = ((bf16[32,8,1152]{2,1,0:T(8,128)(2,1)}), bf16[32,8,1152]{2,1,0:T(8,128)(2,1)S(1)}, u32[]{:S(2)}, u32[]{:S(2)}) async-start(bf16[32,8,1152]{2,1,0:T(8,128)(2,1)} %bitcast.5), calls=%async_computation.1 | async-start | bytes 1179648 | tf_op jit(solution)/shard_map/all_to_all | solution.py:281
  40.6 7.3 %collective-permute-start.4 = (bf16[264,256]{1,0:T(8,128)(2,1)S(1)}, bf16[264,256]{1,0:T(8,128)(2,1)S(1)}, u32[]{:S(2)}, u32[]{:S(2)}) collective-permute-start(bf16[264,256]{1,0:T(8,128)(2,1)S(1)} %get-tuple-element.8), channel_id=1, source_target_pairs={{0,32},{8,40},{16,48},{24,56},{32,64},{40,72},{48,80},{56,88},{64,... | collective-permute-start | bytes 405512 | tf_op jit(solution)/shard_map/ppermute | solution.py:256
  47.9 2.5 %collective-permute-start.3 = (bf16[264,256]{1,0:T(8,128)(2,1)S(1)}, bf16[264,256]{1,0:T(8,128)(2,1)S(1)}, u32[]{:S(2)}, u32[]{:S(2)}) collective-permute-start(bf16[264,256]{1,0:T(8,128)(2,1)S(1)} %get-tuple-element.8), channel_id=1, source_target_pairs={{0,24},{8,32},{16,40},{24,48},{32,56},{64,88},{72,96},{80,104},{88... | collective-permute-start | bytes 405512 | tf_op jit(solution)/shard_map/ppermute | solution.py:260
  50.4 8.2 %collective-permute-start.2 = (bf16[264,256]{1,0:T(8,128)(2,1)S(1)}, bf16[264,256]{1,0:T(8,128)(2,1)S(1)}, u32[]{:S(2)}, u32[]{:S(2)}) collective-permute-start(bf16[264,256]{1,0:T(8,128)(2,1)S(1)} %get-tuple-element.8), channel_id=1, source_target_pairs={{0,16},{8,24},{16,32},{24,40},{32,48},{40,56},{64,80},{72,88},{80,... | collective-permute-start | bytes 405512 | tf_op jit(solution)/shard_map/ppermute | solution.py:260
  58.6 3.4 %collective-permute-start.1 = (bf16[264,256]{1,0:T(8,128)(2,1)S(1)}, bf16[264,256]{1,0:T(8,128)(2,1)S(1)}, u32[]{:S(2)}, u32[]{:S(2)}) collective-permute-start(bf16[264,256]{1,0:T(8,128)(2,1)S(1)} %get-tuple-element.8), channel_id=1, source_target_pairs={{0,8},{8,16},{16,24},{24,32},{32,40},{40,48},{48,56},{64,72},{72,8... | collective-permute-start | bytes 405512 | tf_op jit(solution)/shard_map/ppermute | solution.py:260
  62.0 24.3 %collective-permute-done.4.far = bf16[264,256]{1,0:T(8,128)(2,1)S(1)} collective-permute-done((bf16[264,256]{1,0:T(8,128)(2,1)S(1)}, bf16[264,256]{1,0:T(8,128)(2,1)S(1)}, u32[]{:S(2)}, u32[]{:S(2)}) %collective-permute-start.4) | collective-permute-done | bytes 135200 | tf_op jit(solution)/shard_map/ppermute | solution.py:256
  86.3 1.3 %collective-permute-start.7 = (bf16[264,256]{1,0:T(8,128)(2,1)S(1)}, bf16[264,256]{1,0:T(8,128)(2,1)S(1)}, u32[]{:S(2)}, u32[]{:S(2)}) collective-permute-start(bf16[264,256]{1,0:T(8,128)(2,1)S(1)} %collective-permute-done.4.far), channel_id=1, source_target_pairs={{8,0},{16,8},{24,16},{72,64},{80,72},{88,80},{136,128},{144,136},{... | collective-permute-start | bytes 405512 | tf_op jit(solution)/shard_map/ppermute | solution.py:263
  87.5 1.3 %collective-permute-start.6 = (bf16[264,256]{1,0:T(8,128)(2,1)S(1)}, bf16[264,256]{1,0:T(8,128)(2,1)S(1)}, u32[]{:S(2)}, u32[]{:S(2)}) collective-permute-start(bf16[264,256]{1,0:T(8,128)(2,1)S(1)} %collective-permute-done.4.far), channel_id=1, source_target_pairs={{16,0},{24,8},{80,64},{88,72},{144,128},{152,136},{208,192},{216,2... | collective-permute-start | bytes 405512 | tf_op jit(solution)/shard_map/ppermute | solution.py:263
  88.8 0.0 collective-permute-done.3.b3
  88.9 1.3 %collective-permute-start.5 = (bf16[264,256]{1,0:T(8,128)(2,1)S(1)}, bf16[264,256]{1,0:T(8,128)(2,1)S(1)}, u32[]{:S(2)}, u32[]{:S(2)}) collective-permute-start(bf16[264,256]{1,0:T(8,128)(2,1)S(1)} %collective-permute-done.4.far), channel_id=1, source_target_pairs={{24,0},{88,64},{152,128},{216,192},{25,1},{89,65},{153,129},{217,1... | collective-permute-start | bytes 405512 | tf_op jit(solution)/shard_map/ppermute | solution.py:263
  90.2 0.0 collective-permute-done.2.b2
  90.2 0.0 collective-permute-done.1.b1
  90.2 3.9 %collective-permute-done.7.c3 = bf16[264,256]{1,0:T(8,128)(2,1)S(1)} collective-permute-done((bf16[264,256]{1,0:T(8,128)(2,1)S(1)}, bf16[264,256]{1,0:T(8,128)(2,1)S(1)}, u32[]{:S(2)}, u32[]{:S(2)}) %collective-permute-start.7) | collective-permute-done | bytes 135200 | tf_op jit(solution)/shard_map/ppermute | solution.py:263
  94.0 8.5 %collective-permute-done.6.c2 = bf16[264,256]{1,0:T(8,128)(2,1)S(1)} collective-permute-done((bf16[264,256]{1,0:T(8,128)(2,1)S(1)}, bf16[264,256]{1,0:T(8,128)(2,1)S(1)}, u32[]{:S(2)}, u32[]{:S(2)}) %collective-permute-start.6) | collective-permute-done | bytes 135200 | tf_op jit(solution)/shard_map/ppermute | solution.py:263
  102.6 0.0 collective-permute-done.5.c1
  102.6 0.0 all-to-all-done.1
  102.6 0.0 copy-done.1
  102.6 10.9 %attend.1 = bf16[384,1024]{1,0:T(8,128)(2,1)} custom-call(bf16[256,1280]{1,0:T(8,128)(2,1)S(1)} %bitcast.11, s32[1,384]{1,0:T(1,128)S(1)} %reshape.21.seg_ref, bf16[256,1152]{1,0:T(8,128)(2,1)S(1)} %bitcast.14, bf16[264,256]{1,0:T(8,128)(2,1)S(1)} %collective-permute-done.1.b1, bf16[264,256]{1,0:T(8,128)(2,1)S(1)} %collective-permute-done.2.b2, ...), custom_call_target="tpu_custom_call" | custom-call | flops 6000000000 | bytes 4000000 | tf_op jit(solution)/shard_map/attend/pallas_call | solution.py:283
  (1 shorter events, 0.0 us)
Async XLA Ops:
  0.7 0.7 copy-start.3
  1.3 1.1 copy-start
  2.4 0.9 copy-start.2
  3.4 5.9 %collective-permute-start = (bf16[72,256]{1,0:T(8,128)(2,1)S(1)}, bf16[72,256]{1,0:T(8,128)(2,1)S(1)}, u32[]{:S(2)}, u32[]{:S(2)}) collective-permute-start(bf16[72,256]{1,0:T(8,128)(2,1)S(1)} %get-tuple-element.7), channel_id=1, source_target_pairs={{0,256},{256,512},{512,768},{1,257},{257,513},{513,769},{2,258},{2... | collective-permute-start | bytes 110600 | tf_op jit(solution)/shard_map/ppermute | solution.py:254
  22.1 80.5 %copy-start.1 = (bf16[256,1,1280]{2,0,1:T(8,128)(2,1)S(1)}, bf16[256,1,1280]{2,0,1:T(8,128)(2,1)}, u32[]{:S(2)}) copy-start(bf16[256,1,1280]{2,0,1:T(8,128)(2,1)} %param.4) | copy-start | bytes 1966084
  22.1 80.5 %all-to-all-start.1 = ((bf16[32,8,1152]{2,1,0:T(8,128)(2,1)}), bf16[32,8,1152]{2,1,0:T(8,128)(2,1)S(1)}, u32[]{:S(2)}, u32[]{:S(2)}) async-start(bf16[32,8,1152]{2,1,0:T(8,128)(2,1)} %bitcast.5), calls=%async_computation.1 | async-start | bytes 1179648 | tf_op jit(solution)/shard_map/all_to_all | solution.py:281
  40.6 45.6 %collective-permute-start.4 = (bf16[264,256]{1,0:T(8,128)(2,1)S(1)}, bf16[264,256]{1,0:T(8,128)(2,1)S(1)}, u32[]{:S(2)}, u32[]{:S(2)}) collective-permute-start(bf16[264,256]{1,0:T(8,128)(2,1)S(1)} %get-tuple-element.8), channel_id=1, source_target_pairs={{0,32},{8,40},{16,48},{24,56},{32,64},{40,72},{48,80},{56,88},{64,... | collective-permute-start | bytes 405512 | tf_op jit(solution)/shard_map/ppermute | solution.py:256
  47.9 40.9 %collective-permute-start.3 = (bf16[264,256]{1,0:T(8,128)(2,1)S(1)}, bf16[264,256]{1,0:T(8,128)(2,1)S(1)}, u32[]{:S(2)}, u32[]{:S(2)}) collective-permute-start(bf16[264,256]{1,0:T(8,128)(2,1)S(1)} %get-tuple-element.8), channel_id=1, source_target_pairs={{0,24},{8,32},{16,40},{24,48},{32,56},{64,88},{72,96},{80,104},{88... | collective-permute-start | bytes 405512 | tf_op jit(solution)/shard_map/ppermute | solution.py:260
  50.4 39.8 %collective-permute-start.2 = (bf16[264,256]{1,0:T(8,128)(2,1)S(1)}, bf16[264,256]{1,0:T(8,128)(2,1)S(1)}, u32[]{:S(2)}, u32[]{:S(2)}) collective-permute-start(bf16[264,256]{1,0:T(8,128)(2,1)S(1)} %get-tuple-element.8), channel_id=1, source_target_pairs={{0,16},{8,24},{16,32},{24,40},{32,48},{40,56},{64,80},{72,88},{80,... | collective-permute-start | bytes 405512 | tf_op jit(solution)/shard_map/ppermute | solution.py:260
  58.6 31.6 %collective-permute-start.1 = (bf16[264,256]{1,0:T(8,128)(2,1)S(1)}, bf16[264,256]{1,0:T(8,128)(2,1)S(1)}, u32[]{:S(2)}, u32[]{:S(2)}) collective-permute-start(bf16[264,256]{1,0:T(8,128)(2,1)S(1)} %get-tuple-element.8), channel_id=1, source_target_pairs={{0,8},{8,16},{16,24},{24,32},{32,40},{40,48},{48,56},{64,72},{72,8... | collective-permute-start | bytes 405512 | tf_op jit(solution)/shard_map/ppermute | solution.py:260
  86.3 7.8 %collective-permute-start.7 = (bf16[264,256]{1,0:T(8,128)(2,1)S(1)}, bf16[264,256]{1,0:T(8,128)(2,1)S(1)}, u32[]{:S(2)}, u32[]{:S(2)}) collective-permute-start(bf16[264,256]{1,0:T(8,128)(2,1)S(1)} %collective-permute-done.4.far), channel_id=1, source_target_pairs={{8,0},{16,8},{24,16},{72,64},{80,72},{88,80},{136,128},{144,136},{... | collective-permute-start | bytes 405512 | tf_op jit(solution)/shard_map/ppermute | solution.py:263
  87.5 15.0 %collective-permute-start.6 = (bf16[264,256]{1,0:T(8,128)(2,1)S(1)}, bf16[264,256]{1,0:T(8,128)(2,1)S(1)}, u32[]{:S(2)}, u32[]{:S(2)}) collective-permute-start(bf16[264,256]{1,0:T(8,128)(2,1)S(1)} %collective-permute-done.4.far), channel_id=1, source_target_pairs={{16,0},{24,8},{80,64},{88,72},{144,128},{152,136},{208,192},{216,2... | collective-permute-start | bytes 405512 | tf_op jit(solution)/shard_map/ppermute | solution.py:263
  88.9 13.7 %collective-permute-start.5 = (bf16[264,256]{1,0:T(8,128)(2,1)S(1)}, bf16[264,256]{1,0:T(8,128)(2,1)S(1)}, u32[]{:S(2)}, u32[]{:S(2)}) collective-permute-start(bf16[264,256]{1,0:T(8,128)(2,1)S(1)} %collective-permute-done.4.far), channel_id=1, source_target_pairs={{24,0},{88,64},{152,128},{216,192},{25,1},{89,65},{153,129},{217,1... | collective-permute-start | bytes 405512 | tf_op jit(solution)/shard_map/ppermute | solution.py:263
where the time goes:
time: 114 us; the launch traced here: 113 us
  starting transfers between devices  45 us (39%)
  waiting for transfers between devices  41.3 us (36%)
  Pallas kernels  12.5 us (11%)
  blocking collectives  11.3 us (10%)
  local copies, waits for them, and re-layouts  3.34 us (3%)
    ppermute x1, waiting for transfers between devices, layer(): lax.ppermute(mine, ('group', 'seq'), [(o, o + REACH) for o in range(total...  24.3 us
    all_to_all x1, starting transfers between devices, layer(): lax.all_to_all(packed, 'seq', split_axis=0, concat_axis=0, tiled=True)  18.5 us
    ppermute x3, starting transfers between devices, layer(): near.append(lax.ppermute(mine, 'seq', pairs))  14 us
    ppermute x3, waiting for transfers between devices, layer(): seam.append(lax.ppermute(far, 'seq', pairs))  12.4 us
    all_to_all x1, blocking collectives, layer(): lax.all_to_all(listed, 'shard', split_axis=0, concat_axis=0, tiled=True)  11.3 us
    pallas_call x1, Pallas kernels, layer(): pl.pallas_call(attend_kernel, out_shape=jax.ShapeDtypeStruct((rows, q), B...  10.9 us
    ppermute x1, starting transfers between devices, layer(): lax.ppermute(mine, ('group', 'seq'), [(o, o + REACH) for o in range(total...  7.28 us
    ppermute x1, waiting for transfers between devices, layer(): step = lax.ppermute(step, 'group', [(i, i + 1) for i in range(groups - 1)])  4.55 us
  transfers between devices with their start and end apart: 9, of which 4 were waited for; matrix products, arithmetic and copies ran while one was open for 0% of the time, Pallas kernels for 0%

commit v1 on v0

--- a/solution.py
+++ b/solution.py
@@ -20,7 +20,7 @@
 F32 = jnp.float32
 BF16 = jnp.bfloat16
 
-VARIANTS = (1, 3, 5)
+VARIANTS = (1, 2, 3, 4, 5)
 
 
 def iota(shape, dim):
@@ -39,18 +39,23 @@
     return jnp.where(cond, 1.0, 0.0)
 
 
-def halo_kernel(text_ref, vis_ref, dest_ref, seg_ref, mine_ref, step_ref):
-    text = text_ref.shape[0]
-    block = vis_ref.shape[0]
-    wide = text_ref.shape[1]
-    rows = seg_ref.shape[1]
-    per_dev = dest_ref.shape[1]
+def seg_lanes(seg_ref):
+    return jnp.concatenate([seg_ref[i : i + 1] for i in range(seg_ref.shape[0])], axis=1).astype(F32)
+
+
+def halo_kernel(text_ref, seg_ref, mine_ref):
+    text, wide = text_ref.shape
     mine_ref[:text] = text_ref[...]
-    tags = seg_ref[...].astype(F32) + 1.0
-    pad = jnp.zeros((1, 2 * wide - rows), F32)
+    tags = seg_lanes(seg_ref) + 1.0
+    pad = jnp.zeros((1, 2 * wide - tags.shape[1]), F32)
     tags = jnp.concatenate([tags, pad], axis=1)
     tags = jnp.concatenate([tags[:, :wide], tags[:, wide:], jnp.zeros((6, wide), F32)], axis=0)
     mine_ref[text:] = tags.astype(BF16)
+
+
+def step_kernel(vis_ref, dest_ref, step_ref):
+    block, wide = vis_ref.shape
+    per_dev = dest_ref.shape[1]
     step_ref[:block] = vis_ref[...]
     dest = jnp.concatenate([dest_ref[...].astype(F32), jnp.zeros((1, wide - per_dev), F32)], axis=1)
     step_ref[block:] = jnp.broadcast_to(dest, (8, wide)).astype(BF16)
@@ -128,7 +133,7 @@
     vv[:text, :DH] = text_ref[:, q + DH :]
     vv[text:rows, :DH] = high[:, :DH].astype(BF16)
     vv[:, DH:] = jnp.ones((vv.shape[0], DH), BF16)
-    tags = jnp.broadcast_to(seg_ref[0:1].astype(F32) + 1.0, (8, rows))
+    tags = jnp.broadcast_to(seg_lanes(seg_ref) + 1.0, (8, rows))
     first_tag = tags[0:1, 0:1]
     diag = ones_where(iota((rows, rows), 0) == iota((rows, rows), 1)) * tags[0:1]
     tag_col = dot(diag.astype(BF16), jnp.ones((rows, LANES), BF16))
@@ -229,35 +234,40 @@
     text2 = text_rows.reshape(text, wide)
     vis2 = vis_rows.reshape(block, wide)
     dest = vis_dest.reshape(1, per_dev)
+    segs = segments.reshape(rows // LANES, LANES)
     tail_block = q // (2 * DH)
-    mine, step = pl.pallas_call(
+    step = pl.pallas_call(
+        step_kernel,
+        grid=(1,),
+        in_specs=[
+            pl.BlockSpec((block, 2 * DH), lambda i: (0, tail_block)),
+            pl.BlockSpec((1, per_dev), lambda i: (0, 0)),
+        ],
+        out_specs=pl.BlockSpec((block + 8, 2 * DH), lambda i: (0, 0)),
+        out_shape=jax.ShapeDtypeStruct((block + 8, 2 * DH), BF16),
+        cost_estimate=cost(1000, 70_000),
+        name="step_rows",
+    )(vis2, dest)
+    mine = pl.pallas_call(
         halo_kernel,
         grid=(1,),
         in_specs=[
             pl.BlockSpec((text, 2 * DH), lambda i: (0, tail_block)),
-            pl.BlockSpec((block, 2 * DH), lambda i: (0, tail_block)),
-            pl.BlockSpec((1, per_dev), lambda i: (0, 0)),
-            pl.BlockSpec((1, rows), lambda i: (0, 0)),
+            pl.BlockSpec((rows // LANES, LANES), lambda i: (0, 0)),
         ],
-        out_specs=[
-            pl.BlockSpec((text + 8, 2 * DH), lambda i: (0, 0)),
-            pl.BlockSpec((block + 8, 2 * DH), lambda i: (0, 0)),
-        ],
-        out_shape=[
-            jax.ShapeDtypeStruct((text + 8, 2 * DH), BF16),
-            jax.ShapeDtypeStruct((block + 8, 2 * DH), BF16),
-        ],
+        out_specs=pl.BlockSpec((text + 8, 2 * DH), lambda i: (0, 0)),
+        out_shape=jax.ShapeDtypeStruct((text + 8, 2 * DH), BF16),
         cost_estimate=cost(1000, 300_000),
-        compiler_params=vmem(8),
         name="halo_rows",
-    )(text2, vis2, dest, segments.reshape(1, rows))
+    )(text2, segs)
     step = lax.ppermute(step, "group", [(i, i + 1) for i in range(groups - 1)])
 
     far = lax.ppermute(mine, ("group", "seq"), [(o, o + REACH) for o in range(total - REACH)])
     near, seam = [], []
     for k in range(1, REACH):
-        pairs = [(s, s + k) for s in range(seq_count) if s % RING + k < RING]
-        near.append(lax.ppermute(mine, "seq", pairs))
+        by = 1 if k == REACH - 1 else k
+        pairs = [(s, s + by) for s in range(seq_count) if s % RING + by < RING]
+        near.append(lax.ppermute(near[-1] if by < k else mine, "seq", pairs))
     for k in range(1, REACH):
         pairs = [(s + REACH - k, s) for s in range(seq_count) if s % RING < k]
         seam.append(lax.ppermute(far, "seq", pairs))
@@ -295,7 +305,7 @@
         cost_estimate=cost(6_000_000_000, 4_000_000),
         compiler_params=vmem(32),
         name="attend",
-    )(text2, segments.reshape(1, rows), came, *near, far, *seam)
+    )(text2, segs, came, *near, far, *seam)
     return out.reshape(rows, 1, q)
 
 

time: 114 us -> 111 us (0.974)
  starting transfers between devices: 45 us -> 39.7 us
  waiting for transfers between devices: 41.3 us -> 45.5 us
  local copies, waits for them, and re-layouts: 3.34 us -> 0.02 us
  Pallas kernels: 12.5 us -> 13.7 us
    ppermute x1, waiting for transfers between devices: 24.3 us -> 31.5 us  [layer(): lax.ppermute(mine, ('group', 'seq'), [(o, o + REACH) for o in range(total...]
    ppermute x3, starting transfers between devices: 14 us -> 8.88 us  [layer(): near.append(lax.ppermute(near[-1] if by < k else mine, 'seq', pairs))]
    ppermute x3, waiting for transfers between devices: 12.4 us -> 9.24 us  [layer(): seam.append(lax.ppermute(far, 'seq', pairs))]
    unnamed x8, local copies, waits for them, and re-layouts: 2.66 us -> 0.02 us
    pallas_call x1, Pallas kernels: 10.9 us -> 8.94 us  [layer(): pl.pallas_call(attend_kernel, out_shape=jax.ShapeDtypeStruct((rows, q), B...]
    pallas_call x1, Pallas kernels: 0.02 us -> 1.64 us  [layer(): pl.pallas_call(halo_kernel, grid=(1,), in_specs=[pl.BlockSpec((text, 2 *...]
    pallas_call x0 -> x1, Pallas kernels: none -> 1.45 us  [layer(): pl.pallas_call(step_kernel, grid=(1,), in_specs=[pl.BlockSpec((block, 2 *...]
  transfers between devices with their start and end apart: 9 -> 9, of which waited for: 4 -> 3; matrix products, arithmetic and copies ran while one was open for 0% -> 0% of each run, Pallas kernels for 0% -> 1%
where the time goes in v1:
time: 111 us; the launch traced here: 110 us
  waiting for transfers between devices  45.5 us (41%)
  starting transfers between devices  39.7 us (36%)
  Pallas kernels  13.7 us (12%)
  blocking collectives  11.3 us (10%)
    ppermute x1, waiting for transfers between devices, layer(): lax.ppermute(mine, ('group', 'seq'), [(o, o + REACH) for o in range(total...  31.5 us
    all_to_all x1, starting transfers between devices, layer(): lax.all_to_all(packed, 'seq', split_axis=0, concat_axis=0, tiled=True)  18.4 us
    all_to_all x1, blocking collectives, layer(): lax.all_to_all(listed, 'shard', split_axis=0, concat_axis=0, tiled=True)  11.3 us
    ppermute x3, waiting for transfers between devices, layer(): seam.append(lax.ppermute(far, 'seq', pairs))  9.24 us
    pallas_call x1, Pallas kernels, layer(): pl.pallas_call(attend_kernel, out_shape=jax.ShapeDtypeStruct((rows, q), B...  8.94 us
    ppermute x3, starting transfers between devices, layer(): near.append(lax.ppermute(near[-1] if by < k else mine, 'seq', pairs))  8.88 us
    ppermute x1, starting transfers between devices, layer(): lax.ppermute(mine, ('group', 'seq'), [(o, o + REACH) for o in range(total...  7.27 us
    ppermute x1, waiting for transfers between devices, layer(): step = lax.ppermute(step, 'group', [(i, i + 1) for i in range(groups - 1)])  4.76 us
  transfers between devices with their start and end apart: 9, of which 3 were waited for; matrix products, arithmetic and copies ran while one was open for 0% of the time, Pallas kernels for 1%

profile of v1, /device:TPU:448, one launch (start us, length us, event | category | flops | bytes accessed | tf_op | source)
XLA Modules:
  0.0 110.2 jit_solution(8391339577274985540)
XLA Ops:
  0.0 0.0 copy-start.1
  0.0 0.0 copy-start.3
  0.0 1.5 %step_rows.1 = bf16[72,256]{1,0:T(8,128)(2,1)} custom-call(bf16[64,1280]{1,0:T(8,128)(2,1)} %bitcast.13, s32[1,8]{1,0:T(1,128)} %bitcast.18), custom_call_target="tpu_custom_call" | custom-call | flops 1000 | bytes 70000 | tf_op jit(solution)/shard_map/step_rows/pallas_call | solution.py:239
  1.5 1.3 %collective-permute-start = (bf16[72,256]{1,0:T(8,128)(2,1)}, bf16[72,256]{1,0:T(8,128)(2,1)S(1)}, u32[]{:S(2)}, u32[]{:S(2)}) collective-permute-start(bf16[72,256]{1,0:T(8,128)(2,1)} %step_rows.1), channel_id=1, source_target_pairs={{0,256},{256,512},{512,768},{1,257},{257,513},{513,769},{2,258},{2... | collective-permute-start | bytes 110600 | tf_op jit(solution)/shard_map/ppermute | solution.py:263
  2.7 4.8 %collective-permute-done.step_ref = bf16[72,256]{1,0:T(8,128)(2,1)S(1)} collective-permute-done((bf16[72,256]{1,0:T(8,128)(2,1)}, bf16[72,256]{1,0:T(8,128)(2,1)S(1)}, u32[]{:S(2)}, u32[]{:S(2)}) %collective-permute-start) | collective-permute-done | bytes 36896 | tf_op jit(solution)/shard_map/ppermute | solution.py:263
  7.5 0.0 copy-done.1
  7.5 0.0 copy-done.3
  7.5 0.2 list_rows.1
  7.7 11.3 %all_to_all.22 = bf16[8,8,1792]{2,1,0:T(8,128)(2,1)S(1)} all-to-all(bf16[8,8,1792]{2,1,0:T(8,128)(2,1)S(1)} %bitcast.9), channel_id=1, replica_groups=mesh['group'=4,'seq'=32,'shard'=8] {'shard'}, dimensions={0} | all-to-all | bytes 458752 | tf_op jit(solution)/shard_map/all_to_all | solution.py:282
  19.0 1.4 %pack_rows.1 = bf16[256,1152]{1,0:T(8,128)(2,1)} custom-call(bf16[64,1792]{1,0:T(8,128)(2,1)S(1)} %bitcast.10), custom_call_target="tpu_custom_call" | custom-call | flops 200000000 | bytes 800000 | tf_op jit(solution)/shard_map/pack_rows/pallas_call | solution.py:284
  20.4 18.4 %all-to-all-start.1 = ((bf16[32,8,1152]{2,1,0:T(8,128)(2,1)}), bf16[32,8,1152]{2,1,0:T(8,128)(2,1)S(1)}, u32[]{:S(2)}, u32[]{:S(2)}) async-start(bf16[32,8,1152]{2,1,0:T(8,128)(2,1)} %bitcast.6), calls=%async_computation.1 | async-start | bytes 1179648 | tf_op jit(solution)/shard_map/all_to_all | solution.py:291
  38.8 0.0 copy-start
  38.8 0.0 copy-start.2
  38.8 1.6 %halo_rows.1 = bf16[264,256]{1,0:T(8,128)(2,1)} custom-call(bf16[256,1280]{1,0:T(8,128)(2,1)} %bitcast.11, s32[3,128]{1,0:T(4,128)} %bitcast.16), custom_call_target="tpu_custom_call" | custom-call | flops 1000 | bytes 300000 | tf_op jit(solution)/shard_map/halo_rows/pallas_call | solution.py:251
  40.4 7.3 %collective-permute-start.4 = (bf16[264,256]{1,0:T(8,128)(2,1)}, bf16[264,256]{1,0:T(8,128)(2,1)S(1)}, u32[]{:S(2)}, u32[]{:S(2)}) collective-permute-start(bf16[264,256]{1,0:T(8,128)(2,1)} %halo_rows.1), channel_id=1, source_target_pairs={{0,32},{8,40},{16,48},{24,56},{32,64},{40,72},{48,80},{56,88},{64,... | collective-permute-start | bytes 405512 | tf_op jit(solution)/shard_map/ppermute | solution.py:265
  47.7 2.5 %collective-permute-start.2 = (bf16[264,256]{1,0:T(8,128)(2,1)}, bf16[264,256]{1,0:T(8,128)(2,1)S(1)}, u32[]{:S(2)}, u32[]{:S(2)}) collective-permute-start(bf16[264,256]{1,0:T(8,128)(2,1)} %halo_rows.1), channel_id=1, source_target_pairs={{0,16},{8,24},{16,32},{24,40},{32,48},{40,56},{64,80},{72,88},{80,... | collective-permute-start | bytes 405512 | tf_op jit(solution)/shard_map/ppermute | solution.py:270
  50.2 2.5 %collective-permute-start.1 = (bf16[264,256]{1,0:T(8,128)(2,1)}, bf16[264,256]{1,0:T(8,128)(2,1)S(1)}, u32[]{:S(2)}, u32[]{:S(2)}) collective-permute-start(bf16[264,256]{1,0:T(8,128)(2,1)} %halo_rows.1), channel_id=1, source_target_pairs={{0,8},{8,16},{16,24},{24,32},{32,40},{40,48},{48,56},{64,72},{72,8... | collective-permute-start | bytes 405512 | tf_op jit(solution)/shard_map/ppermute | solution.py:270
  52.7 31.5 %collective-permute-done.4.far = bf16[264,256]{1,0:T(8,128)(2,1)S(1)} collective-permute-done((bf16[264,256]{1,0:T(8,128)(2,1)}, bf16[264,256]{1,0:T(8,128)(2,1)S(1)}, u32[]{:S(2)}, u32[]{:S(2)}) %collective-permute-start.4) | collective-permute-done | bytes 135200 | tf_op jit(solution)/shard_map/ppermute | solution.py:265
  84.1 1.3 %collective-permute-start.7 = (bf16[264,256]{1,0:T(8,128)(2,1)S(1)}, bf16[264,256]{1,0:T(8,128)(2,1)S(1)}, u32[]{:S(2)}, u32[]{:S(2)}) collective-permute-start(bf16[264,256]{1,0:T(8,128)(2,1)S(1)} %collective-permute-done.4.far), channel_id=1, source_target_pairs={{8,0},{16,8},{24,16},{72,64},{80,72},{88,80},{136,128},{144,136},{... | collective-permute-start | bytes 405512 | tf_op jit(solution)/shard_map/ppermute | solution.py:273
  85.4 1.3 %collective-permute-start.6 = (bf16[264,256]{1,0:T(8,128)(2,1)S(1)}, bf16[264,256]{1,0:T(8,128)(2,1)S(1)}, u32[]{:S(2)}, u32[]{:S(2)}) collective-permute-start(bf16[264,256]{1,0:T(8,128)(2,1)S(1)} %collective-permute-done.4.far), channel_id=1, source_target_pairs={{16,0},{24,8},{80,64},{88,72},{144,128},{152,136},{208,192},{216,2... | collective-permute-start | bytes 405512 | tf_op jit(solution)/shard_map/ppermute | solution.py:273
  86.7 1.3 %collective-permute-start.5 = (bf16[264,256]{1,0:T(8,128)(2,1)S(1)}, bf16[264,256]{1,0:T(8,128)(2,1)S(1)}, u32[]{:S(2)}, u32[]{:S(2)}) collective-permute-start(bf16[264,256]{1,0:T(8,128)(2,1)S(1)} %collective-permute-done.4.far), channel_id=1, source_target_pairs={{24,0},{88,64},{152,128},{216,192},{25,1},{89,65},{153,129},{217,1... | collective-permute-start | bytes 405512 | tf_op jit(solution)/shard_map/ppermute | solution.py:273
  88.0 0.0 collective-permute-done.2.b2
  88.0 3.9 %collective-permute-start.3 = (bf16[264,256]{1,0:T(8,128)(2,1)S(1)}, bf16[264,256]{1,0:T(8,128)(2,1)S(1)}, u32[]{:S(2)}, u32[]{:S(2)}) collective-permute-start(bf16[264,256]{1,0:T(8,128)(2,1)S(1)} %collective-permute-done.2.b2), channel_id=1, source_target_pairs={{0,8},{8,16},{16,24},{24,32},{32,40},{40,48},{48,56},{64,72},{72,8... | collective-permute-start | bytes 405512 | tf_op jit(solution)/shard_map/ppermute | solution.py:270
  92.0 0.0 collective-permute-done.1.b1
  92.0 0.0 collective-permute-done.7.c3
  92.0 9.2 %collective-permute-done.6.c2 = bf16[264,256]{1,0:T(8,128)(2,1)S(1)} collective-permute-done((bf16[264,256]{1,0:T(8,128)(2,1)S(1)}, bf16[264,256]{1,0:T(8,128)(2,1)S(1)}, u32[]{:S(2)}, u32[]{:S(2)}) %collective-permute-start.6) | collective-permute-done | bytes 135200 | tf_op jit(solution)/shard_map/ppermute | solution.py:273
  101.2 0.0 collective-permute-done.5.c1
  101.3 0.0 collective-permute-done.3.b3
  101.3 0.0 all-to-all-done.1
  101.3 0.0 copy-done
  101.3 0.0 copy-done.2
  101.3 8.9 %attend.1 = bf16[384,1024]{1,0:T(8,128)(2,1)} custom-call(bf16[256,1280]{1,0:T(8,128)(2,1)S(1)} %bitcast.12, s32[3,128]{1,0:T(4,128)S(1)} %bitcast.17, bf16[256,1152]{1,0:T(8,128)(2,1)S(1)} %bitcast.15, bf16[264,256]{1,0:T(8,128)(2,1)S(1)} %collective-permute-done.1.b1, bf16[264,256]{1,0:T(8,128)(2,1)S(1)} %collective-permute-done.2.b2, ...), custom_call_target="tpu_custom_call" | custom-call | flops 6000000000 | bytes 4000000 | tf_op jit(solution)/shard_map/attend/pallas_call | solution.py:293
Async XLA Ops:
  0.0 7.5 %copy-start.1 = (bf16[8,8,1280]{2,1,0:T(8,128)(2,1)S(1)}, bf16[8,8,1280]{2,1,0:T(8,128)(2,1)}, u32[]{:S(2)}) copy-start(bf16[8,8,1280]{2,1,0:T(8,128)(2,1)} %param.5) | copy-start | bytes 491524
  0.0 7.5 %copy-start.3 = (s32[8,1]{0,1:T(1,128)S(1)}, s32[8,1]{0,1:T(1,128)}, u32[]{:S(2)}) copy-start(s32[8,1]{0,1:T(1,128)} %param.6) | copy-start | bytes 100
  1.5 6.0 %collective-permute-start = (bf16[72,256]{1,0:T(8,128)(2,1)}, bf16[72,256]{1,0:T(8,128)(2,1)S(1)}, u32[]{:S(2)}, u32[]{:S(2)}) collective-permute-start(bf16[72,256]{1,0:T(8,128)(2,1)} %step_rows.1), channel_id=1, source_target_pairs={{0,256},{256,512},{512,768},{1,257},{257,513},{513,769},{2,258},{2... | collective-permute-start | bytes 110600 | tf_op jit(solution)/shard_map/ppermute | solution.py:263
  20.4 80.9 %all-to-all-start.1 = ((bf16[32,8,1152]{2,1,0:T(8,128)(2,1)}), bf16[32,8,1152]{2,1,0:T(8,128)(2,1)S(1)}, u32[]{:S(2)}, u32[]{:S(2)}) async-start(bf16[32,8,1152]{2,1,0:T(8,128)(2,1)} %bitcast.6), calls=%async_computation.1 | async-start | bytes 1179648 | tf_op jit(solution)/shard_map/all_to_all | solution.py:291
  38.8 62.5 %copy-start = (bf16[256,1,1280]{2,0,1:T(8,128)(2,1)S(1)}, bf16[256,1,1280]{2,0,1:T(8,128)(2,1)}, u32[]{:S(2)}) copy-start(bf16[256,1,1280]{2,0,1:T(8,128)(2,1)} %param.4) | copy-start | bytes 1966084
  38.8 62.5 %copy-start.2 = (s32[384]{0:T(512)S(1)}, s32[384]{0:T(512)}, u32[]{:S(2)}) copy-start(s32[384]{0:T(512)} %param.7) | copy-start | bytes 4612
  40.4 43.7 %collective-permute-start.4 = (bf16[264,256]{1,0:T(8,128)(2,1)}, bf16[264,256]{1,0:T(8,128)(2,1)S(1)}, u32[]{:S(2)}, u32[]{:S(2)}) collective-permute-start(bf16[264,256]{1,0:T(8,128)(2,1)} %halo_rows.1), channel_id=1, source_target_pairs={{0,32},{8,40},{16,48},{24,56},{32,64},{40,72},{48,80},{56,88},{64,... | collective-permute-start | bytes 405512 | tf_op jit(solution)/shard_map/ppermute | solution.py:265
  47.7 40.3 %collective-permute-start.2 = (bf16[264,256]{1,0:T(8,128)(2,1)}, bf16[264,256]{1,0:T(8,128)(2,1)S(1)}, u32[]{:S(2)}, u32[]{:S(2)}) collective-permute-start(bf16[264,256]{1,0:T(8,128)(2,1)} %halo_rows.1), channel_id=1, source_target_pairs={{0,16},{8,24},{16,32},{24,40},{32,48},{40,56},{64,80},{72,88},{80,... | collective-permute-start | bytes 405512 | tf_op jit(solution)/shard_map/ppermute | solution.py:270
  50.2 41.8 %collective-permute-start.1 = (bf16[264,256]{1,0:T(8,128)(2,1)}, bf16[264,256]{1,0:T(8,128)(2,1)S(1)}, u32[]{:S(2)}, u32[]{:S(2)}) collective-permute-start(bf16[264,256]{1,0:T(8,128)(2,1)} %halo_rows.1), channel_id=1, source_target_pairs={{0,8},{8,16},{16,24},{24,32},{32,40},{40,48},{48,56},{64,72},{72,8... | collective-permute-start | bytes 405512 | tf_op jit(solution)/shard_map/ppermute | solution.py:270
  84.1 7.9 %collective-permute-start.7 = (bf16[264,256]{1,0:T(8,128)(2,1)S(1)}, bf16[264,256]{1,0:T(8,128)(2,1)S(1)}, u32[]{:S(2)}, u32[]{:S(2)}) collective-permute-start(bf16[264,256]{1,0:T(8,128)(2,1)S(1)} %collective-permute-done.4.far), channel_id=1, source_target_pairs={{8,0},{16,8},{24,16},{72,64},{80,72},{88,80},{136,128},{144,136},{... | collective-permute-start | bytes 405512 | tf_op jit(solution)/shard_map/ppermute | solution.py:273
  85.4 15.8 %collective-permute-start.6 = (bf16[264,256]{1,0:T(8,128)(2,1)S(1)}, bf16[264,256]{1,0:T(8,128)(2,1)S(1)}, u32[]{:S(2)}, u32[]{:S(2)}) collective-permute-start(bf16[264,256]{1,0:T(8,128)(2,1)S(1)} %collective-permute-done.4.far), channel_id=1, source_target_pairs={{16,0},{24,8},{80,64},{88,72},{144,128},{152,136},{208,192},{216,2... | collective-permute-start | bytes 405512 | tf_op jit(solution)/shard_map/ppermute | solution.py:273
  86.7 14.5 %collective-permute-start.5 = (bf16[264,256]{1,0:T(8,128)(2,1)S(1)}, bf16[264,256]{1,0:T(8,128)(2,1)S(1)}, u32[]{:S(2)}, u32[]{:S(2)}) collective-permute-start(bf16[264,256]{1,0:T(8,128)(2,1)S(1)} %collective-permute-done.4.far), channel_id=1, source_target_pairs={{24,0},{88,64},{152,128},{216,192},{25,1},{89,65},{153,129},{217,1... | collective-permute-start | bytes 405512 | tf_op jit(solution)/shard_map/ppermute | solution.py:273
  88.0 13.2 %collective-permute-start.3 = (bf16[264,256]{1,0:T(8,128)(2,1)S(1)}, bf16[264,256]{1,0:T(8,128)(2,1)S(1)}, u32[]{:S(2)}, u32[]{:S(2)}) collective-permute-start(bf16[264,256]{1,0:T(8,128)(2,1)S(1)} %collective-permute-done.2.b2), channel_id=1, source_target_pairs={{0,8},{8,16},{16,24},{24,32},{32,40},{40,48},{48,56},{64,72},{72,8... | collective-permute-start | bytes 405512 | tf_op jit(solution)/shard_map/ppermute | solution.py:270

commit v2 on v1

v2 whole, which is shorter than its diff:
```python
import functools

import jax
import jax.numpy as jnp
from jax import lax
from jax.experimental import pallas as pl
from jax.experimental.pallas import tpu as pltpu
from jax.sharding import PartitionSpec as P


GQ = 8
DH = 128
CAP = 4
REACH = 4
RING = 8
LANES = 128
DEAD = 64.0
BIG = 1e30
SCALE = DH ** (-0.5) * 1.4426950408889634
F32 = jnp.float32
BF16 = jnp.bfloat16


def iota(shape, dim):
    return lax.broadcasted_iota(jnp.int32, shape, dim)


def dot(a, b):
    return jnp.dot(a, b, preferred_element_type=F32)


def dot_nt(a, b):
    return lax.dot_general(a, b, (((1,), (1,)), ((), ())), preferred_element_type=F32)


def ones_where(cond):
    return jnp.where(cond, 1.0, 0.0)


def seg_lanes(seg_ref):
    return jnp.concatenate([seg_ref[i : i + 1] for i in range(seg_ref.shape[0])], axis=1).astype(F32)


def halo_kernel(text_ref, seg_ref, mine_ref):
    text, wide = text_ref.shape
    mine_ref[:text] = text_ref[...]
    tags = seg_lanes(seg_ref) + 1.0
    pad = jnp.zeros((1, 2 * wide - tags.shape[1]), F32)
    tags = jnp.concatenate([tags, pad], axis=1)
    tags = jnp.concatenate([tags[:, :wide], tags[:, wide:], jnp.zeros((6, wide), F32)], axis=0)
    mine_ref[text:] = tags.astype(BF16)


def step_kernel(vis_ref, dest_ref, step_ref):
    block, wide = vis_ref.shape
    per_dev = dest_ref.shape[1]
    step_ref[:block] = vis_ref[...]
    dest = jnp.concatenate([dest_ref[...].astype(F32), jnp.zeros((1, wide - per_dev), F32)], axis=1)
    step_ref[block:] = jnp.broadcast_to(dest, (8, wide)).astype(BF16)


def row_move(per_dev, heads):
    count = per_dev * heads
    a, b = iota((count, count), 0), iota((count, count), 1)
    move = ones_where(b == (a % per_dev) * heads + a // per_dev).astype(BF16)
    return move, iota((count, per_dev), 1) == iota((count, per_dev), 0) % per_dev


def spread(pick, dest):
    dest = jnp.sum(jnp.where(pick, dest, 0.0), axis=1, keepdims=True)
    return jnp.broadcast_to(dest, (pick.shape[0], LANES)).astype(BF16)


def list_kernel(per_dev, heads, rows_ref, dest_ref, out_ref):
    wide = rows_ref.shape[1]
    move, pick = row_move(per_dev, heads)
    out_ref[:, :wide] = dot(move, rows_ref[...]).astype(BF16)
    out_ref[:, wide : wide + LANES] = spread(pick, dest_ref[...].astype(F32))


def add_kernel(per_dev, heads, step_ref, listed_ref, out_ref):
    count = per_dev * heads
    wide = listed_ref.shape[1]
    move, pick = row_move(per_dev, heads)
    out_ref[:, :wide] = listed_ref[...]
    out_ref[:, wide : wide + 2 * DH] = dot(move, step_ref[:count]).astype(BF16)
    out_ref[:, wide + 2 * DH :] = spread(pick, step_ref[count : count + 1, :per_dev].astype(F32))


def slot_row(named):
    count = named.shape[0]
    onehot = ones_where(named.astype(F32).astype(jnp.int32) == iota((count, LANES), 1)).astype(BF16)
    same = dot_nt(onehot, onehot)
    a, b = iota((count, count), 0), iota((count, count), 1)
    rank = jnp.sum(jnp.where(a < b, same, 0.0), axis=0, keepdims=True)
    dest = dot_nt(iota((8, LANES), 1).astype(F32).astype(BF16), onehot)[0:1]
    return dest * CAP + rank


def pack_kernel(own_ref, out_ref):
    count = own_ref.shape[0]
    rows = out_ref.shape[0]
    slot_count = rows // 2
    q = GQ * DH
    wide = q + 2 * DH
    slots = slot_row(own_ref[:, wide : wide + LANES])
    before = slot_row(own_ref[:, wide + LANES + 2 * DH :]) - slot_count
    both = jnp.concatenate([slots, before], axis=1)
    kv = jnp.concatenate([own_ref[:, q:wide], own_ref[:, wide + LANES : wide + LANES + 2 * DH]], axis=0)
    r = iota((rows, count), 0)
    sid = ((r // 8) * CAP + r % CAP).astype(F32)
    low = (r % 8) < CAP
    put0 = ones_where(low & (sid == slots))
    put1 = ones_where((~low) & (sid == slots))
    base = dot(put0.astype(BF16), own_ref[:, : q + DH])
    fill0 = jnp.sum(put0, axis=1, keepdims=True)
    first = base[:, :DH] + dot(put1.astype(BF16), own_ref[:, q + DH : wide])
    fill = fill0 + jnp.sum(put1, axis=1, keepdims=True)
    out_ref[:, :DH] = jnp.where(fill > 0, first, DEAD).astype(BF16)
    r = iota((rows, 2 * count), 0)
    sid = ((r // 8) * CAP + r % CAP).astype(F32)
    low = (r % 8) < CAP
    for k in range(1, REACH + 1):
        put = ones_where((~low) & (sid - CAP * k == both))
        lo = DH + 2 * DH * (k - 1)
        val = base[:, lo : lo + 2 * DH] + dot(put.astype(BF16), kv)
        fill = fill0 + jnp.sum(put, axis=1, keepdims=True)
        out_ref[:, lo : lo + 2 * DH] = jnp.where(fill > 0, val, DEAD).astype(BF16)


def by_blocks(used, run):
    for blocks in range(1, REACH + 2):

        @pl.when(used + 1 == blocks)
        def _(blocks=blocks):
            run(blocks)


PAIR = 2


def over_pairs(score, weigh, bufs):
    count = GQ // PAIR

    def two(i, top):
        u = 2 * i
        after = score(u + 1, bufs[1])
        weigh(u, bufs[0], top)
        top = score(jnp.minimum(u + 2, count - 1), bufs[0])
        weigh(u + 1, bufs[1], after)
        return top

    lax.fori_loop(0, count // 2, two, score(0, bufs[0]))


def pair_rows(ref, u, extra):
    got = ref[:, pl.ds(pl.multiple_of(u * PAIR * DH, PAIR * DH), PAIR * DH)]
    both = jnp.concatenate([got[:, :DH], got[:, DH:]], axis=0)
    return jnp.concatenate([both, jnp.concatenate([extra, extra], axis=0)], axis=1)


def twice(x):
    return jnp.concatenate([x, x], axis=0)


def row_max(parts):
    top = None
    for s in parts:
        for i in range(s.shape[1] // LANES):
            part = s[:, i * LANES : (i + 1) * LANES]
            top = part if top is None else jnp.maximum(top, part)
    return jnp.max(top, axis=1, keepdims=True)


def text_kernel(
    text_ref, seg_ref, b1, b2, b3, far, c1, c2, c3, part_ref, ml_ref, kvt, qx, bias_ref, counts_ref, kt, vt, bias_t, sa, sb
):
    text = text_ref.shape[0]
    rows = qx.shape[0]
    vis = rows - text
    q = GQ * DH
    kt[:text, :DH] = text_ref[:, q : q + DH]
    kt[:text, DH:] = jnp.zeros((text, LANES), BF16)
    vt[:text, :DH] = text_ref[:, q + DH :]
    vt[:, DH:] = jnp.ones((vt.shape[0], DH), BF16)
    kvt[:text] = text_ref[:, q:]
    tags = jnp.broadcast_to(seg_lanes(seg_ref) + 1.0, (8, rows))
    first_tag = tags[0:1, 0:1]
    diag = ones_where(iota((rows, rows), 0) == iota((rows, rows), 1)) * tags[0:1]
    tag_col = dot(diag.astype(BF16), jnp.ones((rows, LANES), BF16))
    a, b = iota((text, text), 0), iota((text, text), 1)
    wide = jnp.concatenate([tag_col[:text]] * (text // LANES), axis=1)
    bias_t[...] = jnp.where((b <= a) & (wide == tags[0:1, :text]), 0.0, -BIG)
    a, b = iota((vis, rows), 0) + text, iota((vis, rows), 1)
    wide = jnp.concatenate([tag_col[text:]] * (rows // LANES), axis=1)
    bias_ref[...] = jnp.where((b <= a) & (wide == tags[0:1]), 0.0, -BIG)
    lane = iota((rows, LANES), 1)
    row_bias = jnp.where(tag_col == first_tag, 0.0, -BIG)
    qx[...] = jnp.where(lane == 0, 1.0, jnp.where(lane == 1, row_bias, 0.0)).astype(BF16)
    place_r = iota((text, LANES), 0).astype(F32)
    counts = []
    for k in range(1, REACH + 1):
        ref = far[...] if k == REACH else (b1, b2, b3)[k - 1][...] + (c1, c2, c3)[k - 1][...]
        same = ones_where(ref[text : text + 8, :].astype(F32) == first_tag)
        count = jnp.sum(same[0:1] + same[1:2], axis=1, keepdims=True)
        at = k * text
        kt[at : at + text, :DH] = ref[:text, :DH]
        vt[at : at + text, :DH] = ref[:text, DH:]
        kvt[at : at + text] = ref[:text]
        ok = jnp.where(place_r >= rows - count, 0.0, -BIG)
        kt[at : at + text, DH:] = jnp.where(lane[:text] == 0, ok, ones_where(lane[:text] == 1)).astype(BF16)
        counts.append(jnp.broadcast_to(count, (1, LANES)))
    counts = jnp.concatenate(counts + [jnp.zeros((8 - REACH, LANES), F32)], axis=0)
    counts_ref[...] = counts
    used = jnp.sum(ones_where(counts[:, :1] > 0.5)).astype(jnp.int32)

    def run(blocks):
        def score(u, ss):
            qe = pair_rows(text_ref, u, qx[:text])
            parts = []
            for k in range(blocks):
                s = dot_nt(qe, kt[k * text : (k + 1) * text])
                if k == 0:
                    s = s + twice(bias_t[...])
                ss[:, k * text : (k + 1) * text] = s
                parts.append(s)
            return row_max(parts)

        def weigh(u, ss, top):
            p = jnp.exp2((ss[:, : blocks * text] - top) * SCALE).astype(BF16)
            acc = dot(p, vt[: blocks * text])
            at = pl.multiple_of(u * PAIR * DH, PAIR * DH)
            part_ref[:, pl.ds(at, PAIR * DH)] = jnp.concatenate([acc[:text, :DH], acc[text:, :DH]], axis=1)
            lane = iota((text, LANES), 1)
            first = jnp.where(lane < 32, top[:text], acc[:text, DH:])
            second = jnp.where(lane < 96, top[text:], acc[text:, DH:])
            ml_ref[:, pl.ds(pl.multiple_of(u * LANES, LANES), LANES)] = jnp.where(lane < 64, first, second)

        over_pairs(score, weigh, (sa, sb))

    by_blocks(used, run)


def join_kernel(
    text_hbm, came_ref, part_ref, ml_ref, kvt, qx, bias_ref, counts_ref, out_hbm, text_ref, out_ref, sem_in, sem_out, qv, kt, vt, kv, vv, bias_v, va, ta, vb, tb
):
    text = text_hbm.shape[0]
    load = pltpu.make_async_copy(text_hbm.at[:, : GQ * DH], text_ref, sem_in)
    load.start()
    vis = came_ref.shape[0] // 2
    rows = text + vis
    q = GQ * DH
    a, b = iota((2 * vis, 2 * vis), 0), iota((2 * vis, 2 * vis), 1)
    src = ((a % vis) // CAP) * 8 + a % CAP + CAP * (a // vis)
    both = dot(ones_where(b == src).astype(BF16), came_ref[...])
    low, high = both[:vis], both[vis:]
    qv[...] = low[:, :q].astype(BF16)
    own_k = low[:, q:].astype(BF16)
    kv[:vis, :DH] = own_k
    kv[:vis, DH:] = jnp.zeros((vis, LANES), BF16)
    vv[:vis, :DH] = high[:, :DH].astype(BF16)
    vv[:, DH:] = jnp.ones((vv.shape[0], DH), BF16)
    pick0 = ones_where(iota((8, DH), 1) == 0).astype(BF16)
    own_live = dot_nt(pick0, own_k)[0:1] < DEAD / 2
    bias_v[:, :text] = bias_ref[:, :text]
    bias_v[:, text:] = jnp.where(own_live, bias_ref[:, text:], -BIG)
    live_q = jnp.broadcast_to(ones_where(low[:, q : q + 1] < DEAD / 2), (vis, LANES)) > 0.5
    used = jnp.sum(ones_where(counts_ref[:, :1] > 0.5)).astype(jnp.int32)
    lane = iota((vis, LANES), 1)
    place_r = (iota((vis, LANES), 0) + text).astype(F32)
    lane_t, place_t = iota((text, LANES), 1), iota((text, LANES), 0).astype(F32)
    kt[:, :DH] = kvt[:, :DH]
    kt[:text, DH:] = jnp.zeros((text, LANES), BF16)
    vt[:, :DH] = kvt[:, DH:]
    vt[:, DH:] = jnp.ones((vt.shape[0], DH), BF16)
    for k in range(1, REACH + 1):
        start = rows - counts_ref[k - 1 : k]
        lo = DH + 2 * DH * (k - 1)
        pk = high[:, lo : lo + DH]
        at = k * vis
        kv[at : at + vis, :DH] = pk.astype(BF16)
        vv[at : at + vis, :DH] = high[:, lo + DH : lo + 2 * DH].astype(BF16)
        live = jnp.broadcast_to(ones_where(pk[:, 0:1] < DEAD / 2), (vis, LANES)) > 0.5
        ok = (place_r >= start) & live
        kv[at : at + vis, DH:] = jnp.where(lane == 0, jnp.where(ok, 0.0, -BIG), ones_where(lane == 1)).astype(BF16)
        ok = jnp.where(place_t >= start, 0.0, -BIG)
        kt[k * text : (k + 1) * text, DH:] = jnp.where(lane_t == 0, ok, ones_where(lane_t == 1)).astype(BF16)

    load.wait()

    def run(blocks):
        split = blocks * text
        end = blocks * rows

        def score(u, bufs):
            ss, ts = bufs
            qe = pair_rows(qv, u, qx[text:])
            parts = []
            for k in range(blocks):
                s = dot_nt(qe, kt[k * text : (k + 1) * text])
                if k == 0:
                    s = s + twice(bias_v[:, :text])
                ss[:, k * text : (k + 1) * text] = s
                parts.append(s)
            s = dot_nt(qe, kv[:vis]) + twice(bias_v[:, text:])
            ss[:, split : split + vis] = s
            parts.append(s)
            if blocks > 1:
                s = dot_nt(qe, kv[vis : blocks * vis])
                ss[:, split + vis : end] = s
                parts.append(s)
            top_v = row_max(parts)
            ml = ml_ref[:, pl.ds(pl.multiple_of(u * LANES, LANES), LANES)]
            top_t = jnp.concatenate([ml[:, :1], ml[:, 64:65]], axis=0)
            if blocks > 1:
                s = dot_nt(pair_rows(text_ref, u, qx[:text]), kv[vis : blocks * vis])
                ts[:, : (blocks - 1) * vis] = s
                top_t = jnp.maximum(row_max([s]), top_t)
            return top_v, top_t

        def weigh(u, bufs, tops):
            ss, ts = bufs
            top_v, top_t = tops
            at = pl.multiple_of(u * PAIR * DH, PAIR * DH)
            p = jnp.exp2((ss[:, :end] - top_v) * SCALE).astype(BF16)
            acc = dot(p[:, :split], vt[:split]) + dot(p[:, split:], vv[: blocks * vis])
            out = acc[:, :DH] / acc[:, DH:]
            out = jnp.concatenate([jnp.where(live_q, out[:vis], 0.0), jnp.where(live_q, out[vis:], 0.0)], axis=1)
            out_ref[text:, pl.ds(at, PAIR * DH)] = out.astype(BF16)
            part = part_ref[:, pl.ds(at, PAIR * DH)]
            num = jnp.concatenate([part[:, :DH], part[:, DH:]], axis=0)
            ml = ml_ref[:, pl.ds(pl.multiple_of(u * LANES, LANES), LANES)]
            den = jnp.broadcast_to(jnp.concatenate([ml[:, 32:33], ml[:, 96:97]], axis=0), num.shape)
            if blocks > 1:
                p = jnp.exp2((ts[:, : (blocks - 1) * vis] - top_t) * SCALE).astype(BF16)
                was = jnp.concatenate([ml[:, :1], ml[:, 64:65]], axis=0)
                fade = jnp.broadcast_to(jnp.exp2((was - top_t) * SCALE), num.shape)
                acc = dot(p, vv[vis : blocks * vis])
                num = num * fade + acc[:, :DH]
                den = den * fade + acc[:, DH:]
            out = num / den
            out_ref[:text, pl.ds(at, PAIR * DH)] = jnp.concatenate([out[:text], out[text:]], axis=1).astype(BF16)
            place = pl.ds(at, PAIR * DH)
            pltpu.make_async_copy(out_ref.at[:, place], out_hbm.at[:, place], sem_out.at[u]).start()

        over_pairs(score, weigh, ((va, ta), (vb, tb)))
        for u in range(GQ // PAIR):
            place = pl.ds(u * PAIR * DH, PAIR * DH)
            pltpu.make_async_copy(out_ref.at[:, place], out_hbm.at[:, place], sem_out.at[u]).wait()

    by_blocks(used, run)


def cost(flops, nbytes):
    return pl.CostEstimate(flops=flops, bytes_accessed=nbytes, transcendentals=0)


def vmem(mib):
    return pltpu.CompilerParams(vmem_limit_bytes=mib << 20)


def layer(text_rows, vis_rows, vis_dest, segments):
    seq_count = lax.axis_size("seq")
    groups = lax.axis_size("group")
    text, _, wide = text_rows.shape
    per_dev, heads, _ = vis_rows.shape
    block = per_dev * heads
    vis = seq_count * CAP
    rows = text + vis
    q = GQ * DH
    total = groups * seq_count

    text2 = text_rows.reshape(text, wide)
    vis2 = vis_rows.reshape(block, wide)
    dest = vis_dest.reshape(1, per_dev)
    text_hbm = pltpu.with_memory_space_constraint(text2, pltpu.HBM)
    segs = segments.reshape(rows // LANES, LANES)
    tail_block = q // (2 * DH)
    step = pl.pallas_call(
        step_kernel,
        grid=(1,),
        in_specs=[
            pl.BlockSpec((block, 2 * DH), lambda i: (0, tail_block)),
            pl.BlockSpec((1, per_dev), lambda i: (0, 0)),
        ],
        out_specs=pl.BlockSpec((block + 8, 2 * DH), lambda i: (0, 0)),
        out_shape=jax.ShapeDtypeStruct((block + 8, 2 * DH), BF16),
        cost_estimate=cost(1000, 70_000),
        name="step_rows",
    )(vis2, dest)
    listed = pl.pallas_call(
        functools.partial(list_kernel, per_dev, heads),
        out_shape=jax.ShapeDtypeStruct((block, wide + LANES), BF16),
        cost_estimate=cost(15_000_000, 400_000),
        compiler_params=vmem(8),
        name="list_rows",
    )(vis2, dest)
    mine = pl.pallas_call(
        halo_kernel,
        grid=(1,),
        in_specs=[
            pl.BlockSpec((text, 2 * DH), lambda i: (0, tail_block)),
            pl.BlockSpec((rows // LANES, LANES), lambda i: (0, 0)),
        ],
        out_specs=pl.BlockSpec((text + 8, 2 * DH), lambda i: (0, 0)),
        out_shape=jax.ShapeDtypeStruct((text + 8, 2 * DH), BF16),
        cost_estimate=cost(1000, 300_000),
        name="halo_rows",
    )(text2, segs)
    step = lax.ppermute(step, "group", [(i, i + 1) for i in range(groups - 1)])

    far = lax.ppermute(mine, ("group", "seq"), [(o, o + REACH) for o in range(total - REACH)])
    near, seam = [], []
    for k in range(1, REACH):
        by = 1 if k == REACH - 1 else k
        pairs = [(s, s + by) for s in range(seq_count) if s % RING + by < RING]
        near.append(lax.ppermute(near[-1] if by < k else mine, "seq", pairs))
    for k in range(1, REACH):
        pairs = [(s + REACH - k, s) for s in range(seq_count) if s % RING < k]
        seam.append(lax.ppermute(far, "seq", pairs))

    listed = pl.pallas_call(
        functools.partial(add_kernel, per_dev, heads),
        out_shape=jax.ShapeDtypeStruct((block, wide + 2 * DH + 2 * LANES), BF16),
        cost_estimate=cost(2_000_000, 100_000),
        compiler_params=vmem(8),
        name="add_step",
    )(step, listed)
    own = lax.all_to_all(listed, "shard", split_axis=0, concat_axis=0, tiled=True)

    packed = pl.pallas_call(
        pack_kernel,
        out_shape=jax.ShapeDtypeStruct((seq_count * 8, DH + 2 * DH * REACH), BF16),
        cost_estimate=cost(200_000_000, 800_000),
        compiler_params=vmem(12),
        name="pack_rows",
    )(own)
    came = lax.all_to_all(packed, "seq", split_axis=0, concat_axis=0, tiled=True)

    keys = (REACH + 1) * text
    parts = pl.pallas_call(
        text_kernel,
        out_shape=[
            jax.ShapeDtypeStruct((text, q), F32),
            jax.ShapeDtypeStruct((text, q // PAIR), F32),
            jax.ShapeDtypeStruct((keys, 2 * DH), BF16),
            jax.ShapeDtypeStruct((rows, LANES), BF16),
            jax.ShapeDtypeStruct((vis, rows), F32),
            jax.ShapeDtypeStruct((8, LANES), F32),
        ],
        scratch_shapes=[
            pltpu.VMEM((keys, DH + LANES), BF16),
            pltpu.VMEM((keys, 2 * DH), BF16),
            pltpu.VMEM((text, text), F32),
            pltpu.VMEM((PAIR * text, keys), F32),
            pltpu.VMEM((PAIR * text, keys), F32),
        ],
        cost_estimate=cost(3_000_000_000, 4_000_000),
        compiler_params=vmem(20),
        name="attend_text",
    )(text_hbm, segs, *near, far, *seam)
    out = pl.pallas_call(
        join_kernel,
        out_shape=jax.ShapeDtypeStruct((rows, q), BF16),
        in_specs=[pl.BlockSpec(memory_space=pltpu.HBM)] + [pl.BlockSpec(memory_space=pltpu.VMEM)] * 7,
        out_specs=pl.BlockSpec(memory_space=pltpu.HBM),
        scratch_shapes=[
            pltpu.VMEM((text, q), BF16),
            pltpu.VMEM((rows, q), BF16),
            pltpu.SemaphoreType.DMA,
            pltpu.SemaphoreType.DMA((GQ // PAIR,)),
            pltpu.VMEM((vis, q), BF16),
            pltpu.VMEM((keys, DH + LANES), BF16),
            pltpu.VMEM((keys, 2 * DH), BF16),
            pltpu.VMEM(((REACH + 1) * vis, DH + LANES), BF16),
            pltpu.VMEM(((REACH + 1) * vis, 2 * DH), BF16),
            pltpu.VMEM((vis, rows), F32),
            pltpu.VMEM((PAIR * vis, (REACH + 1) * rows), F32),
            pltpu.VMEM((PAIR * text, REACH * vis), F32),
            pltpu.VMEM((PAIR * vis, (REACH + 1) * rows), F32),
            pltpu.VMEM((PAIR * text, REACH * vis), F32),
        ],
        cost_estimate=cost(3_000_000_000, 4_000_000),
        compiler_params=vmem(20),
        name="attend_join",
    )(text_hbm, came, *parts)
    return out.reshape(rows, 1, q)


def solution(mesh):
    placed = (
        P(("group", "seq"), "shard", None),
        P(("group", "seq", "shard"), None, None),
        P(("group", "seq", "shard"), None),
        P(("group", "seq")),
    )
    return jax.shard_map(
        layer,
        mesh=mesh,
        in_specs=placed,
        out_specs=P(("group", "seq"), "shard", None),
        check_vma=False,
    )
```

time: 111 us -> 114 us (1.027)
  the two profiles are of different devices: /device:TPU:448 before, /device:TPU:457 now
where the time goes in v2:
time: 114 us; the launch traced here: 113 us
  starting transfers between devices  42.4 us (37%)
  waiting for transfers between devices  41.5 us (36%)
  Pallas kernels  17.1 us (15%)
  blocking collectives  12.1 us (11%)
    ppermute x1, waiting for transfers between devices, layer(): lax.ppermute(mine, ('group', 'seq'), [(o, o + REACH) for o in range(total...  29.6 us
    all_to_all x1, starting transfers between devices, layer(): lax.all_to_all(packed, 'seq', split_axis=0, concat_axis=0, tiled=True)  17.7 us
    ppermute x3, starting transfers between devices, layer(): near.append(lax.ppermute(near[-1] if by < k else mine, 'seq', pairs))  12.9 us
    all_to_all x1, blocking collectives, layer(): lax.all_to_all(listed, 'shard', split_axis=0, concat_axis=0, tiled=True)  12.1 us
    ppermute x3, waiting for transfers between devices, layer(): seam.append(lax.ppermute(far, 'seq', pairs))  8.43 us
    pallas_call x1, Pallas kernels, layer(): pl.pallas_call(join_kernel, out_shape=jax.ShapeDtypeStruct((rows, q), BF1...  6.64 us
    ppermute x1, starting transfers between devices, layer(): lax.ppermute(mine, ('group', 'seq'), [(o, o + REACH) for o in range(total...  6.09 us
    pallas_call x1, Pallas kernels, layer(): pl.pallas_call(text_kernel, out_shape=[jax.ShapeDtypeStruct((text, q), F3...  5.73 us
  transfers between devices with their start and end apart: 9, of which 4 were waited for; matrix products, arithmetic and copies ran while one was open for 0% of the time, Pallas kernels for 7%

profile of v2, /device:TPU:457, one launch (start us, length us, event | category | flops | bytes accessed | tf_op | source)
XLA Modules:
  0.0 113.4 jit_solution(13254769515155881112)
XLA Ops:
  0.0 0.0 copy-start
  0.0 0.0 copy-start.2
  0.0 1.5 %step_rows.1 = bf16[72,256]{1,0:T(8,128)(2,1)} custom-call(bf16[64,1280]{1,0:T(8,128)(2,1)} %bitcast.11, s32[1,8]{1,0:T(1,128)} %bitcast.16), custom_call_target="tpu_custom_call" | custom-call | flops 1000 | bytes 70000 | tf_op jit(solution)/shard_map/step_rows/pallas_call | solution.py:379
  1.5 1.3 %collective-permute-start = (bf16[72,256]{1,0:T(8,128)(2,1)}, bf16[72,256]{1,0:T(8,128)(2,1)S(1)}, u32[]{:S(2)}, u32[]{:S(2)}) collective-permute-start(bf16[72,256]{1,0:T(8,128)(2,1)} %step_rows.1), channel_id=1, source_target_pairs={{0,256},{256,512},{512,768},{1,257},{257,513},{513,769},{2,258},{2... | collective-permute-start | bytes 110600 | tf_op jit(solution)/shard_map/ppermute | solution.py:410
  2.7 0.0 copy-done
  2.8 0.0 copy-done.2
  2.8 0.2 list_rows.1.listed_ref
  2.9 3.4 %collective-permute-done.step_ref = bf16[72,256]{1,0:T(8,128)(2,1)S(1)} collective-permute-done((bf16[72,256]{1,0:T(8,128)(2,1)}, bf16[72,256]{1,0:T(8,128)(2,1)S(1)}, u32[]{:S(2)}, u32[]{:S(2)}) %collective-permute-start) | collective-permute-done | bytes 36896 | tf_op jit(solution)/shard_map/ppermute | solution.py:410
  6.4 0.1 add_step.1
  6.5 12.1 %all_to_all.22 = bf16[8,8,1792]{2,1,0:T(8,128)(2,1)S(1)} all-to-all(bf16[8,8,1792]{2,1,0:T(8,128)(2,1)S(1)} %bitcast.9), channel_id=1, replica_groups=mesh['group'=4,'seq'=32,'shard'=8] {'shard'}, dimensions={0} | all-to-all | bytes 458752 | tf_op jit(solution)/shard_map/all_to_all | solution.py:429
  18.6 1.4 %pack_rows.1 = bf16[256,1152]{1,0:T(8,128)(2,1)} custom-call(bf16[64,1792]{1,0:T(8,128)(2,1)S(1)} %bitcast.10), custom_call_target="tpu_custom_call" | custom-call | flops 200000000 | bytes 800000 | tf_op jit(solution)/shard_map/pack_rows/pallas_call | solution.py:431
  20.0 17.7 %all-to-all-start.1 = ((bf16[32,8,1152]{2,1,0:T(8,128)(2,1)}), bf16[32,8,1152]{2,1,0:T(8,128)(2,1)S(1)}, u32[]{:S(2)}, u32[]{:S(2)}) async-start(bf16[32,8,1152]{2,1,0:T(8,128)(2,1)} %bitcast.5), calls=%async_computation.1 | async-start | bytes 1179648 | tf_op jit(solution)/shard_map/all_to_all | solution.py:438
  37.7 0.0 copy-start.1
  37.7 1.6 %halo_rows.1 = bf16[264,256]{1,0:T(8,128)(2,1)} custom-call(bf16[256,1280]{1,0:T(8,128)(2,1)} %bitcast.18, s32[3,128]{1,0:T(4,128)} %bitcast.14), custom_call_target="tpu_custom_call" | custom-call | flops 1000 | bytes 300000 | tf_op jit(solution)/shard_map/halo_rows/pallas_call | solution.py:398
  39.3 6.1 %collective-permute-start.4 = (bf16[264,256]{1,0:T(8,128)(2,1)}, bf16[264,256]{1,0:T(8,128)(2,1)S(1)}, u32[]{:S(2)}, u32[]{:S(2)}) collective-permute-start(bf16[264,256]{1,0:T(8,128)(2,1)} %halo_rows.1), channel_id=1, source_target_pairs={{0,32},{8,40},{16,48},{24,56},{32,64},{40,72},{48,80},{56,88},{64,... | collective-permute-start | bytes 405512 | tf_op jit(solution)/shard_map/ppermute | solution.py:412
  45.4 2.2 %collective-permute-start.2 = (bf16[264,256]{1,0:T(8,128)(2,1)}, bf16[264,256]{1,0:T(8,128)(2,1)S(1)}, u32[]{:S(2)}, u32[]{:S(2)}) collective-permute-start(bf16[264,256]{1,0:T(8,128)(2,1)} %halo_rows.1), channel_id=1, source_target_pairs={{0,16},{8,24},{16,32},{24,40},{32,48},{40,56},{64,80},{72,88},{80,... | collective-permute-start | bytes 405512 | tf_op jit(solution)/shard_map/ppermute | solution.py:417
  47.6 7.0 %collective-permute-start.1 = (bf16[264,256]{1,0:T(8,128)(2,1)}, bf16[264,256]{1,0:T(8,128)(2,1)S(1)}, u32[]{:S(2)}, u32[]{:S(2)}) collective-permute-start(bf16[264,256]{1,0:T(8,128)(2,1)} %halo_rows.1), channel_id=1, source_target_pairs={{0,8},{8,16},{16,24},{24,32},{32,40},{40,48},{48,56},{64,72},{72,8... | collective-permute-start | bytes 405512 | tf_op jit(solution)/shard_map/ppermute | solution.py:417
  54.6 29.6 %collective-permute-done.4.far = bf16[264,256]{1,0:T(8,128)(2,1)S(1)} collective-permute-done((bf16[264,256]{1,0:T(8,128)(2,1)}, bf16[264,256]{1,0:T(8,128)(2,1)S(1)}, u32[]{:S(2)}, u32[]{:S(2)}) %collective-permute-start.4) | collective-permute-done | bytes 135200 | tf_op jit(solution)/shard_map/ppermute | solution.py:412
  84.2 0.7 collective-permute-start.5
  84.9 1.3 %collective-permute-start.6 = (bf16[264,256]{1,0:T(8,128)(2,1)S(1)}, bf16[264,256]{1,0:T(8,128)(2,1)S(1)}, u32[]{:S(2)}, u32[]{:S(2)}) collective-permute-start(bf16[264,256]{1,0:T(8,128)(2,1)S(1)} %collective-permute-done.4.far), channel_id=1, source_target_pairs={{16,0},{24,8},{80,64},{88,72},{144,128},{152,136},{208,192},{216,2... | collective-permute-start | bytes 405512 | tf_op jit(solution)/shard_map/ppermute | solution.py:420
  86.2 2.5 %collective-permute-start.7 = (bf16[264,256]{1,0:T(8,128)(2,1)S(1)}, bf16[264,256]{1,0:T(8,128)(2,1)S(1)}, u32[]{:S(2)}, u32[]{:S(2)}) collective-permute-start(bf16[264,256]{1,0:T(8,128)(2,1)S(1)} %collective-permute-done.4.far), channel_id=1, source_target_pairs={{8,0},{16,8},{24,16},{72,64},{80,72},{88,80},{136,128},{144,136},{... | collective-permute-start | bytes 405512 | tf_op jit(solution)/shard_map/ppermute | solution.py:420
  88.7 0.0 collective-permute-done.2.b2
  88.7 3.7 %collective-permute-start.3 = (bf16[264,256]{1,0:T(8,128)(2,1)S(1)}, bf16[264,256]{1,0:T(8,128)(2,1)S(1)}, u32[]{:S(2)}, u32[]{:S(2)}) collective-permute-start(bf16[264,256]{1,0:T(8,128)(2,1)S(1)} %collective-permute-done.2.b2), channel_id=1, source_target_pairs={{0,8},{8,16},{16,24},{24,32},{32,40},{40,48},{48,56},{64,72},{72,8... | collective-permute-start | bytes 405512 | tf_op jit(solution)/shard_map/ppermute | solution.py:417
  92.4 0.0 collective-permute-done.1.b1
  92.4 0.0 collective-permute-done.5.c1
  92.4 1.5 %collective-permute-done.6.c2 = bf16[264,256]{1,0:T(8,128)(2,1)S(1)} collective-permute-done((bf16[264,256]{1,0:T(8,128)(2,1)S(1)}, bf16[264,256]{1,0:T(8,128)(2,1)S(1)}, u32[]{:S(2)}, u32[]{:S(2)}) %collective-permute-start.6) | collective-permute-done | bytes 135200 | tf_op jit(solution)/shard_map/ppermute | solution.py:420
  93.9 6.9 %collective-permute-done.7.c3 = bf16[264,256]{1,0:T(8,128)(2,1)S(1)} collective-permute-done((bf16[264,256]{1,0:T(8,128)(2,1)S(1)}, bf16[264,256]{1,0:T(8,128)(2,1)S(1)}, u32[]{:S(2)}, u32[]{:S(2)}) %collective-permute-start.7) | collective-permute-done | bytes 135200 | tf_op jit(solution)/shard_map/ppermute | solution.py:420
  100.8 0.0 collective-permute-done.3.b3
  100.9 0.0 copy-done.1
  100.9 5.7 %attend_text.1 = (f32[256,1024]{1,0:T(8,128)S(1)}, f32[256,512]{1,0:T(8,128)S(1)}, bf16[1280,256]{1,0:T(8,128)(2,1)S(1)}, bf16[384,128]{1,0:T(8,128)(2,1)S(1)}, ...) custom-call(bf16[256,1280]{1,0:T(8,128)(2,1)} %bitcast.19, s32[3,128]{1,0:T(4,128)S(1)} %bitcast.15, ...), custom_call_target="tpu_custom_call" | custom-call | flops 3000000000 | bytes 4000000 | tf_op jit(solution)/shard_map/attend_text/pallas_call | solution.py:441
  106.6 0.0 all-to-all-done.1
  106.6 6.6 %attend_join.1 = bf16[384,1024]{1,0:T(8,128)(2,1)} custom-call(bf16[256,1280]{1,0:T(8,128)(2,1)} %bitcast.20, bf16[256,1152]{1,0:T(8,128)(2,1)S(1)} %bitcast.13, f32[256,1024]{1,0:T(8,128)S(1)} %get-tuple-element.11.part_ref, f32[256,512]{1,0:T(8,128)S(1)} %get-tuple-element.12.ml_ref, bf16[1280,256]{1,0:T(8,128)(2,1)S(1)} %get-tuple-element.13.kvt, ...), custom_call_target="tpu_custom_call" | custom-call | flops 3000000000 | bytes 4000000 | tf_op jit(solution)/shard_map/attend_join/pallas_call | solution.py:462
Async XLA Ops:
  0.0 2.7 %copy-start = (bf16[8,8,1280]{2,1,0:T(8,128)(2,1)S(1)}, bf16[8,8,1280]{2,1,0:T(8,128)(2,1)}, u32[]{:S(2)}) copy-start(bf16[8,8,1280]{2,1,0:T(8,128)(2,1)} %param.5) | copy-start | bytes 491524
  0.0 2.8 %copy-start.2 = (s32[8,1]{0,1:T(1,128)S(1)}, s32[8,1]{0,1:T(1,128)}, u32[]{:S(2)}) copy-start(s32[8,1]{0,1:T(1,128)} %param.6) | copy-start | bytes 100
  1.5 4.9 %collective-permute-start = (bf16[72,256]{1,0:T(8,128)(2,1)}, bf16[72,256]{1,0:T(8,128)(2,1)S(1)}, u32[]{:S(2)}, u32[]{:S(2)}) collective-permute-start(bf16[72,256]{1,0:T(8,128)(2,1)} %step_rows.1), channel_id=1, source_target_pairs={{0,256},{256,512},{512,768},{1,257},{257,513},{513,769},{2,258},{2... | collective-permute-start | bytes 110600 | tf_op jit(solution)/shard_map/ppermute | solution.py:410
  20.0 86.6 %all-to-all-start.1 = ((bf16[32,8,1152]{2,1,0:T(8,128)(2,1)}), bf16[32,8,1152]{2,1,0:T(8,128)(2,1)S(1)}, u32[]{:S(2)}, u32[]{:S(2)}) async-start(bf16[32,8,1152]{2,1,0:T(8,128)(2,1)} %bitcast.5), calls=%async_computation.1 | async-start | bytes 1179648 | tf_op jit(solution)/shard_map/all_to_all | solution.py:438
  37.7 63.1 %copy-start.1 = (s32[384]{0:T(512)S(1)}, s32[384]{0:T(512)}, u32[]{:S(2)}) copy-start(s32[384]{0:T(512)} %param.7) | copy-start | bytes 4612
  39.3 44.9 %collective-permute-start.4 = (bf16[264,256]{1,0:T(8,128)(2,1)}, bf16[264,256]{1,0:T(8,128)(2,1)S(1)}, u32[]{:S(2)}, u32[]{:S(2)}) collective-permute-start(bf16[264,256]{1,0:T(8,128)(2,1)} %halo_rows.1), channel_id=1, source_target_pairs={{0,32},{8,40},{16,48},{24,56},{32,64},{40,72},{48,80},{56,88},{64,... | collective-permute-start | bytes 405512 | tf_op jit(solution)/shard_map/ppermute | solution.py:412
  45.4 43.3 %collective-permute-start.2 = (bf16[264,256]{1,0:T(8,128)(2,1)}, bf16[264,256]{1,0:T(8,128)(2,1)S(1)}, u32[]{:S(2)}, u32[]{:S(2)}) collective-permute-start(bf16[264,256]{1,0:T(8,128)(2,1)} %halo_rows.1), channel_id=1, source_target_pairs={{0,16},{8,24},{16,32},{24,40},{32,48},{40,56},{64,80},{72,88},{80,... | collective-permute-start | bytes 405512 | tf_op jit(solution)/shard_map/ppermute | solution.py:417
  47.6 44.8 %collective-permute-start.1 = (bf16[264,256]{1,0:T(8,128)(2,1)}, bf16[264,256]{1,0:T(8,128)(2,1)S(1)}, u32[]{:S(2)}, u32[]{:S(2)}) collective-permute-start(bf16[264,256]{1,0:T(8,128)(2,1)} %halo_rows.1), channel_id=1, source_target_pairs={{0,8},{8,16},{16,24},{24,32},{32,40},{40,48},{48,56},{64,72},{72,8... | collective-permute-start | bytes 405512 | tf_op jit(solution)/shard_map/ppermute | solution.py:417
  84.2 8.2 %collective-permute-start.5 = (bf16[264,256]{1,0:T(8,128)(2,1)S(1)}, bf16[264,256]{1,0:T(8,128)(2,1)S(1)}, u32[]{:S(2)}, u32[]{:S(2)}) collective-permute-start(bf16[264,256]{1,0:T(8,128)(2,1)S(1)} %collective-permute-done.4.far), channel_id=1, source_target_pairs={{24,0},{88,64},{152,128},{216,192},{25,1},{89,65},{153,129},{217,1... | collective-permute-start | bytes 405512 | tf_op jit(solution)/shard_map/ppermute | solution.py:420
  84.9 9.1 %collective-permute-start.6 = (bf16[264,256]{1,0:T(8,128)(2,1)S(1)}, bf16[264,256]{1,0:T(8,128)(2,1)S(1)}, u32[]{:S(2)}, u32[]{:S(2)}) collective-permute-start(bf16[264,256]{1,0:T(8,128)(2,1)S(1)} %collective-permute-done.4.far), channel_id=1, source_target_pairs={{16,0},{24,8},{80,64},{88,72},{144,128},{152,136},{208,192},{216,2... | collective-permute-start | bytes 405512 | tf_op jit(solution)/shard_map/ppermute | solution.py:420
  86.2 14.7 %collective-permute-start.7 = (bf16[264,256]{1,0:T(8,128)(2,1)S(1)}, bf16[264,256]{1,0:T(8,128)(2,1)S(1)}, u32[]{:S(2)}, u32[]{:S(2)}) collective-permute-start(bf16[264,256]{1,0:T(8,128)(2,1)S(1)} %collective-permute-done.4.far), channel_id=1, source_target_pairs={{8,0},{16,8},{24,16},{72,64},{80,72},{88,80},{136,128},{144,136},{... | collective-permute-start | bytes 405512 | tf_op jit(solution)/shard_map/ppermute | solution.py:420
  88.7 12.2 %collective-permute-start.3 = (bf16[264,256]{1,0:T(8,128)(2,1)S(1)}, bf16[264,256]{1,0:T(8,128)(2,1)S(1)}, u32[]{:S(2)}, u32[]{:S(2)}) collective-permute-start(bf16[264,256]{1,0:T(8,128)(2,1)S(1)} %collective-permute-done.2.b2), channel_id=1, source_target_pairs={{0,8},{8,16},{16,24},{24,32},{32,40},{40,48},{48,56},{64,72},{72,8... | collective-permute-start | bytes 405512 | tf_op jit(solution)/shard_map/ppermute | solution.py:417
